TPU v7x, 32 devices: a whole 2x2x4 slice. The times are simulated.
32 devices in a mesh: shard: 8 (over z, y), rep: 4 (over x, core).
Axes of the slice: x: 2, y: 2, z: 4, core: 2. Of those that a mesh axis runs over, the one named last changes fastest.
Arguments:
- queries: bfloat16 [4, 8, 32, 128], P('rep', 'shard'), may hold values from -0.5 to 0.5
- candidates: int32 [4, 8, 64], P('rep', 'shard'), may hold values from 0 to 127, all different within a row; in each aligned block of 8 rows (0 to 7, 8 to 15, ..., all dimensions but the last counted through in order) at most 8 rows name the same one
- codebook: bfloat16 [32768, 128], P(('shard', 'rep')), may hold values from -0.5 to 0.5
- bucket_weights: float32 [4], replicated, may hold values from -0.1 to 0.1
- centroid_ids: int32 [128, 128], P('shard'), may hold values from 0 to 4095
- residual_codes: int32 [128, 128, 128], P('shard'), may hold values from 0 to 3
- passage_lengths: int32 [128], P('shard'), may hold values from 1 to 128, 12288 in all
Outputs:
- best_centroid: float32 [4, 8, 32], P('rep', 'shard')
- scores: float32 [4, 8, 64], P('rep', 'shard')
Inputs may be any that keep to these rules, and one draw needn't show every extreme that they name: `candidates`: each query names 64 different passages. Within the 8 queries of one index of rep, no passage is named by more than 8 queries, a bound that some block reaches. `passage_lengths`: some passage has all 128 slots live.
All inputs are finite; a program needn't handle non-finite values. No bound on the sum of `passage_lengths` on one device may be relied on, other than what follows from the above.
Results may differ from a plain program's by a relative error of at most 0.00045.
Values may be sent and summed in bfloat16 or wider, within the bound.
No kernel may reach another device: no remote copies, remote signals or barrier semaphores. Data moves between devices by JAX's collectives and lax.ppermute only.
A program may use at most 64 MiB of HBM per device.

v0:
```python
import math

import jax
import jax.numpy as jnp
from jax import lax
from jax.sharding import PartitionSpec as P

FAR_BELOW = -1e30


def on_device(
    queries, candidates, codebook, bucket_weights, centroid_ids, residual_codes, passage_lengths
):
    feature_width = queries.shape[3]
    query_len = queries.shape[2]
    per_device = queries.shape[1]
    shard_count = lax.axis_size("shard")
    group_queries, group_cands = (
        lax.all_gather(queries, "shard", axis=1, tiled=True),
        lax.all_gather(candidates, "shard", axis=1, tiled=True),
    )
    group_queries = group_queries[0]
    group_cands = group_cands[0]
    group_size = group_queries.shape[0]
    shard_book = lax.all_gather(codebook, "rep", axis=0, tiled=True)
    token_rows = group_queries.reshape(group_size * query_len, feature_width)
    block_rows = math.gcd(token_rows.shape[0], 512)

    def best_block(row_block):
        scored = jnp.dot(row_block, shard_book.T, preferred_element_type=jnp.float32)
        return jnp.max(scored, axis=1)

    partial_best = lax.map(best_block, token_rows.reshape(-1, block_rows, feature_width)).reshape(
        group_size, query_len
    )
    pass_count, pass_len = centroid_ids.shape
    centre_rows = jnp.take(shard_book, centroid_ids.reshape(-1), axis=0).reshape(
        pass_count, pass_len, feature_width
    )
    residual = jnp.zeros(residual_codes.shape, jnp.float32)
    for bucket in range(bucket_weights.shape[0]):
        residual = residual + jnp.where(residual_codes == bucket, bucket_weights[bucket], 0.0)
    decoded = (centre_rows.astype(jnp.float32) + residual).astype(jnp.bfloat16)
    live_mask = jnp.arange(pass_len, dtype=jnp.int32)[None, :] < passage_lengths[:, None]
    flat_tokens = decoded.reshape(pass_count * pass_len, feature_width)
    block_queries = math.gcd(group_size, max(1, 512 // query_len))

    def dense_block(query_block):
        similar = jnp.dot(
            query_block.reshape(-1, feature_width),
            flat_tokens.T,
            preferred_element_type=jnp.float32,
        )
        similar = similar.reshape(block_queries, query_len, pass_count, pass_len)
        similar = jnp.where(live_mask[None, None], similar, FAR_BELOW)
        return jnp.sum(jnp.max(similar, axis=3), axis=1)

    score_table = lax.map(
        dense_block, group_queries.reshape(-1, block_queries, query_len, feature_width)
    ).reshape(group_size, pass_count)
    own_cands = candidates[0]
    got_best, got_table = (
        lax.all_to_all(partial_best, "shard", split_axis=0, concat_axis=1, tiled=True),
        lax.all_to_all(score_table, "shard", split_axis=0, concat_axis=1, tiled=True),
    )
    own_best = jnp.max(got_best.reshape(per_device, shard_count, query_len), axis=1)
    own_scores = jnp.take_along_axis(got_table, own_cands, axis=1)
    return (own_best[None], own_scores[None])


def solution(mesh):
    in_specs = (
        P("rep", "shard", None, None),
        P("rep", "shard", None),
        P(("shard", "rep"), None),
        P(),
        P("shard", None),
        P("shard", None, None),
        P("shard"),
    )
    out_specs = (P("rep", "shard", None), P("rep", "shard", None))
    return jax.shard_map(
        on_device, mesh=mesh, in_specs=in_specs, out_specs=out_specs, check_vma=False
    )
```

profile of v0, /device:TPU:0, one launch (start us, length us, event | category | flops | bytes accessed | tf_op | source)
XLA Modules:
  0.0 89.6 jit_solution(9013408534027391301)
XLA Ops:
  7.2 0.0 all-gather.2.cloned.1.call-start
  7.2 0.7 all-gather.2.cloned.1.call-update
  7.9 32.6 %all_gather.6 = bf16[1,8,32,128]{3,2,0,1:T(8,128)(2,1)S(1)} all-gather(bf16[1,1,32,128]{3,2,0,1:T(8,128)(2,1)} %bitcast.43), channel_id=1, replica_groups=mesh['shard'=8,'rep'=4] {'shard'}, dimensions={1}, use_global_device_ids=true | all-gather | bytes 73728 | tf_op jit(solution)/shard_map/all_gather | solution.py:19
  40.5 0.7 fusion.1
  41.1 1.5 %fusion.2 = (f32[1]{0:T(128)}, f32[1]{0:T(128)}, f32[1]{0:T(128)}, f32[1]{0:T(128)}) fusion(f32[4]{0:T(128)} %param.10), kind=kLoop, calls=%fused_computation.17 | loop fusion | bytes 32 | tf_op jit(solution)/shard_map/slice | solution.py:42
  42.6 0.7 iota_compare_fusion
  43.3 0.7 compare_and_fusion
  44.0 0.7 compare_select_fusion
  44.8 0.0 copy-start.1
  44.8 0.0 all-gather.2.cloned.1.call-done
  44.8 7.0 %gather_fusion = bf16[2048,128]{1,0:T(8,128)(2,1)S(1)} fusion(bf16[4096,128]{1,0:T(8,128)(2,1)} %all-gather.2.cloned.1.call-done, s32[2048]{0:T(1024)S(1)} %broadcast_clamp_fusion), kind=kCustom, calls=%fused_computation | custom fusion | bytes 1056768 | tf_op jit(solution)/shard_map/jit(_take)/gather | solution.py:37
  51.8 0.0 copy-done.1
  51.9 3.2 %add_convert_fusion = bf16[16,128,128]{2,1,0:T(8,128)(2,1)S(1)} fusion(s32[16,128,128]{2,1,0:T(8,128)S(1)} %copy-done.1, f32[]{:T(128)} %bitcast.10, f32[]{:T(128)} %bitcast.9, f32[]{:T(128)} %bitcast.8, f32[]{:T(128)} %bitcast.7, bf16[16,128,128]{2,1,0:T(8,128)(2,1)S(1)} %bitcast.36, pred[16,128]{1,0:T(8,128)(4,1)S(1)} %compare_and_fusion), kind=kLoop, calls=%fused_computation.6 | loop fusion | flops 3932160 | bytes 2099216 | tf_op jit(solution)/shard_map/convert_element_type | solution.py:43
  55.0 0.4 convolution_bitcast_fusion
  55.4 1.9 %copy.18 = f32[256,2048]{1,0:T(8,128)} copy(f32[256,2048]{0,1:T(8,128)S(1)} %convolution_bitcast_fusion) | data formatting | bytes 4194304 | tf_op jit(solution)/shard_map/while/body/eval_jaxpr/dot_general | solution.py:49
  57.3 2.0 %copy.22 = f32[32,8,16,128]{3,2,1,0:T(8,128)S(1)} copy(f32[32,8,16,128]{3,1,2,0:T(8,128)} %bitcast.35) | data formatting | bytes 4194304
  59.3 0.0 copy-start
  59.3 0.0 copy-start.2
  59.3 0.6 fusion
  59.9 0.6 reduce_sum.10
  60.6 5.5 %all-to-all-start.1 = ((f32[8,1,16]{2,1,0:T(1,128)}), f32[8,1,16]{2,1,0:T(1,128)S(1)}, u32[]{:S(2)}, u32[]{:S(2)}) async-start(f32[8,1,16]{2,1,0:T(1,128)} %bitcast.14), calls=%async_computation.1 | async-start | bytes 8192 | tf_op jit(solution)/shard_map/all_to_all | solution.py:64
  66.1 0.8 convolution_reduce_fusion
  66.8 0.7 all_to_all.22
  67.5 5.0 %all-to-all-done.1 = f32[8,1,16]{2,1,0:T(1,128)S(1)} async-done(((f32[8,1,16]{2,1,0:T(1,128)}), f32[8,1,16]{2,1,0:T(1,128)S(1)}, u32[]{:S(2)}, u32[]{:S(2)}) %all-to-all-start.1) | async-done | bytes 544 | tf_op jit(solution)/shard_map/all_to_all | solution.py:64
  72.5 3.2 %all-to-all-start = ((f32[8,1,32]{2,1,0:T(1,128)}), f32[8,1,32]{2,1,0:T(1,128)S(1)}, u32[]{:S(2)}, u32[]{:S(2)}) async-start(f32[8,1,32]{2,1,0:T(1,128)} %all_to_all.22), calls=%async_computation | async-start | bytes 8192 | tf_op jit(solution)/shard_map/all_to_all | solution.py:63
  75.8 0.5 broadcast.103
  76.3 0.7 reduce.6
  77.0 0.1 reshape.183
  77.1 0.8 gather_fusion.1
  77.8 0.5 and_select_fusion
  78.4 3.9 %all-to-all-done = f32[8,1,32]{2,1,0:T(1,128)S(1)} async-done(((f32[8,1,32]{2,1,0:T(1,128)}), f32[8,1,32]{2,1,0:T(1,128)S(1)}, u32[]{:S(2)}, u32[]{:S(2)}) %all-to-all-start) | async-done | bytes 1056 | tf_op jit(solution)/shard_map/all_to_all | solution.py:63
  82.2 0.5 reduce_max.30
  (4 shorter events, 0.0 us)
Async XLA Ops:
  7.2 37.6 %all-gather.2.cloned.1.call-start = ((), (), s32[]{:S(2)}) async-start(), calls=%async_computation.2 | async-start | bytes 1310720 | tf_op jit(solution)/shard_map/all_gather | solution.py:25
  44.8 7.1 %copy-start.1 = (s32[16,128,128]{2,1,0:T(8,128)S(1)}, s32[16,128,128]{2,1,0:T(8,128)}, u32[]{:S(2)}) copy-start(s32[16,128,128]{2,1,0:T(8,128)} %param.12) | copy-start | bytes 3145732
  59.3 6.8 %copy-start = (bf16[4096,128]{1,0:T(8,128)(2,1)S(1)}, bf16[4096,128]{1,0:T(8,128)(2,1)}, u32[]{:S(2)}) copy-start(bf16[4096,128]{1,0:T(8,128)(2,1)} %all-gather.2.cloned.1.call-done) | copy-start | bytes 3145732
  59.3 18.5 %copy-start.2 = (s32[1,1,64]{2,1,0:T(1,128)S(1)}, s32[1,1,64]{2,1,0:T(1,128)}, u32[]{:S(2)}) copy-start(s32[1,1,64]{2,1,0:T(1,128)} %param.8) | copy-start | bytes 772
  60.6 12.0 %all-to-all-start.1 = ((f32[8,1,16]{2,1,0:T(1,128)}), f32[8,1,16]{2,1,0:T(1,128)S(1)}, u32[]{:S(2)}, u32[]{:S(2)}) async-start(f32[8,1,16]{2,1,0:T(1,128)} %bitcast.14), calls=%async_computation.1 | async-start | bytes 8192 | tf_op jit(solution)/shard_map/all_to_all | solution.py:64
  72.5 9.7 %all-to-all-start = ((f32[8,1,32]{2,1,0:T(1,128)}), f32[8,1,32]{2,1,0:T(1,128)S(1)}, u32[]{:S(2)}, u32[]{:S(2)}) async-start(f32[8,1,32]{2,1,0:T(1,128)} %all_to_all.22), calls=%async_computation | async-start | bytes 8192 | tf_op jit(solution)/shard_map/all_to_all | solution.py:63
Sparse Core Ops, SparseCore 0:
  9.5 19.4 all-gather.1
where the time goes:
time: 90 us; the launch traced here: 89.6 us
  blocking collectives  32.6 us (36%)
  local copies, waits for them, and re-layouts  14.4 us (16%)
  between operations  14.1 us (16%)
  waiting for transfers between devices  9.59 us (11%)
  other arithmetic  8.9 us (10%)
  starting transfers between devices  8.78 us (10%)
  matrix products  1.21 us (1%)
    all_gather x1, blocking collectives, on_device(): lax.all_gather(queries, 'shard', axis=1, tiled=True)  32.6 us
    gather x1, local copies, waits for them, and re-layouts, on_device(): jnp.take(shard_book, centroid_ids.reshape(-1), axis=0)  7.04 us
    all_to_all x1, starting transfers between devices, on_device(): lax.all_to_all(score_table, 'shard', split_axis=0, concat_axis=1, tiled=T...  5.5 us
    all_to_all x1, waiting for transfers between devices, on_device(): lax.all_to_all(score_table, 'shard', split_axis=0, concat_axis=1, tiled=T...  5.02 us
    all_to_all x1, waiting for transfers between devices, on_device(): lax.all_to_all(partial_best, 'shard', split_axis=0, concat_axis=1, tiled=...  3.87 us
    all_to_all x1, starting transfers between devices, on_device(): lax.all_to_all(partial_best, 'shard', split_axis=0, concat_axis=1, tiled=...  3.25 us
    convert_element_type x1, other arithmetic, on_device(): decoded = (centre_rows.astype(jnp.float32) + residual).astype(jnp.bfloat16)  3.16 us
    unnamed x7, local copies, waits for them, and re-layouts  1.99 us
  transfers between devices with their start and end apart: 3, of which 2 were waited for; matrix products, arithmetic and copies ran while one was open for 9% of the time, Pallas kernels for 0%

commit v1 on v0

v1 whole, which is shorter than its diff:
```python
import functools

import jax
import jax.numpy as jnp
from jax import lax
from jax.experimental import pallas as pl
from jax.experimental.pallas import tpu as pltpu
from jax.sharding import PartitionSpec as P

FAR_BELOW = -1e30
LANES = 128
LOW = 256
EXACT = lax.Precision.HIGHEST


def exchange(value, axis, mask):
    count = lax.axis_size(axis)
    return lax.ppermute(value, axis, [(i, i ^ mask) for i in range(count)])


def gather_by_xor(block, axis):
    count = lax.axis_size(axis)
    held = block[None]
    reach = 1
    while reach < count:
        step = 2 if reach == 1 or reach * 2 == count else 4
        parts = [exchange(held, axis, reach * k) for k in range(1, step)]
        held = jnp.concatenate([held] + parts, axis=0)
        reach *= step
    return held


def embed_kernel(rep_ref, weight_ref, ids_ref, codes_ref, *refs):
    *book_refs, out_ref, onehot_ref, high_ref, sum_ref = refs
    passages, slots = ids_ref.shape
    block_rows = book_refs[0].shape[0]
    rows = passages * slots
    ids_by_slot = jnp.transpose(ids_ref[...])
    lane = lax.broadcasted_iota(jnp.int32, (slots, LANES), 1)
    levels = weight_ref.shape[0]
    for p in range(passages):
        here = pl.ds(p * slots, slots)
        ids = jnp.broadcast_to(ids_by_slot[:, p : p + 1], (slots, LANES))
        low = ids & (LOW - 1)
        onehot_ref[here, :] = jnp.concatenate(
            [(low == lane + k * LANES).astype(jnp.float32) for k in range(LOW // LANES)], axis=1
        ).astype(jnp.bfloat16)
        high_ref[here, :] = ids >> (LOW.bit_length() - 1)
        sum_ref[here, :] = jnp.zeros((slots, LANES), jnp.float32)
    chunk = slots
    for k, book_ref in enumerate(book_refs):
        first = (rep_ref[0] ^ k) * (block_rows // LOW)
        for j in range(0, block_rows // LOW, 2):
            pair = jnp.concatenate(
                [book_ref[(j + h) * LOW : (j + h + 1) * LOW, :] for h in range(2)], axis=1
            )
            for c in range(rows // chunk):
                here = pl.ds(c * chunk, chunk)
                found = jnp.dot(onehot_ref[here, :], pair, preferred_element_type=jnp.float32)
                high = high_ref[here, :]
                total = sum_ref[here, :]
                for h in range(2):
                    total = jnp.where(high == first + (j + h), found[:, h * LANES : (h + 1) * LANES], total)
                sum_ref[here, :] = total
    for p in range(passages):
        here = pl.ds(p * slots, slots)
        codes = codes_ref[p]
        residual = jnp.full(codes.shape, weight_ref[levels - 1], jnp.float32)
        for level in range(levels - 2, -1, -1):
            residual = jnp.where(codes == level, weight_ref[level], residual)
        out_ref[here, :] = (sum_ref[here, :] + residual).astype(jnp.bfloat16)


def score_kernel(tokens, shard_ref, length_ref, query_ref, embedded_ref, *refs):
    *book_refs, out_ref = refs
    passages = length_ref.shape[0]
    slots = embedded_ref.shape[0] // passages
    width = query_ref.shape[0]
    count = width // tokens
    queries = query_ref[...]

    def product(rows):
        return lax.dot_general(
            rows, queries, (((1,), (1,)), ((), ())), preferred_element_type=jnp.float32
        )

    best = jnp.full((8, width), FAR_BELOW, jnp.float32)
    chunk = 128
    for book_ref in book_refs:
        for c in range(book_ref.shape[0] // chunk):
            found = product(book_ref[c * chunk : (c + 1) * chunk, :])
            best = jnp.maximum(best, jnp.max(found.reshape(chunk // 8, 8, width), axis=0))
    best = jnp.max(best, axis=0, keepdims=True)
    slot = lax.broadcasted_iota(jnp.int32, (slots, width), 0)
    tops = []
    for p in range(passages):
        found = product(embedded_ref[p * slots : (p + 1) * slots, :])
        found = jnp.where(slot < length_ref[p], found, FAR_BELOW)
        tops.append(jnp.max(found, axis=0, keepdims=True))
    lane_room = out_ref.shape[1]
    table = jnp.concatenate(
        [jnp.zeros((tokens, width), jnp.float32)]
        + tops
        + [jnp.zeros((lane_room - tokens - passages, width), jnp.float32)],
        axis=0,
    )
    mine = (
        lax.broadcasted_iota(jnp.int32, (count, width), 1) // tokens
        == lax.broadcasted_iota(jnp.int32, (count, width), 0)
    ).astype(jnp.float32)
    sums = lax.dot_general(
        mine, table, (((1,), (1,)), ((), ())), preferred_element_type=jnp.float32, precision=EXACT
    )
    start = pl.program_id(0) * count
    for q in range(count):
        row = pl.ds((start + q) ^ shard_ref[0], 1)
        out_ref[row, :] = sums[q : q + 1, :]
        out_ref[row, 0:tokens] = best[:, q * tokens : (q + 1) * tokens]


def finish_kernel(tokens, passages, table_ref, cands_ref, best_ref, scores_ref):
    table = table_ref[...]
    shards, room = table.shape
    best_ref[...] = jnp.max(table, axis=0, keepdims=True)[:, 0:tokens]
    cands = cands_ref[...]
    count = cands.shape[1]
    owner = (lax.broadcasted_iota(jnp.int32, (shards, count), 0) == cands // passages).astype(jnp.float32)
    columns = lax.dot_general(
        table, owner, (((0,), (0,)), ((), ())), preferred_element_type=jnp.float32, precision=EXACT
    )
    wanted = lax.broadcasted_iota(jnp.int32, (room, count), 0) == tokens + cands % passages
    scores_ref[...] = jnp.sum(jnp.where(wanted, columns, 0.0), axis=0, keepdims=True)


def on_device(queries, candidates, codebook, bucket_weights, centroid_ids, residual_codes, passage_lengths):
    tokens, features = queries.shape[2:]
    passages, slots = centroid_ids.shape
    shards, reps = lax.axis_size("shard"), lax.axis_size("rep")
    vmem = pl.BlockSpec(memory_space=pltpu.VMEM)
    smem = pl.BlockSpec(memory_space=pltpu.SMEM)
    shard = lax.axis_index("shard").astype(jnp.int32).reshape(1)
    rep = lax.axis_index("rep").astype(jnp.int32).reshape(1)

    books = {0: codebook}
    bit = reps // 2
    while bit:
        for k in list(books):
            books[k ^ bit] = exchange(books[k], "rep", bit)
        bit //= 2
    books = [books[k] for k in range(reps)]
    group = gather_by_xor(queries[0, 0], "shard").reshape(shards * tokens, features)

    rows = passages * slots
    embedded = pl.pallas_call(
        embed_kernel,
        out_shape=jax.ShapeDtypeStruct((rows, features), jnp.bfloat16),
        in_specs=[smem, smem] + [vmem] * (2 + reps),
        out_specs=vmem,
        scratch_shapes=[
            pltpu.VMEM((rows, LOW), jnp.bfloat16),
            pltpu.VMEM((rows, LANES), jnp.int32),
            pltpu.VMEM((rows, features), jnp.float32),
        ],
        compiler_params=pltpu.CompilerParams(vmem_limit_bytes=24 << 20),
        cost_estimate=pl.CostEstimate(flops=2 * rows * LOW * features * 16, bytes_accessed=2 << 20, transcendentals=0),
    )(rep, bucket_weights, centroid_ids, residual_codes, *books)

    room = -(-(tokens + passages) // LANES) * LANES
    width = 256
    packed = pl.pallas_call(
        functools.partial(score_kernel, tokens),
        out_shape=jax.ShapeDtypeStruct((shards, room), jnp.float32),
        grid=(shards * tokens // width,),
        in_specs=[smem, smem, pl.BlockSpec((width, features), lambda i: (i, 0))] + [vmem] * (1 + reps),
        out_specs=vmem,
        compiler_params=pltpu.CompilerParams(vmem_limit_bytes=24 << 20),
        cost_estimate=pl.CostEstimate(flops=2 * 6144 * 256 * features, bytes_accessed=2 << 20, transcendentals=0),
    )(shard, passage_lengths, group, embedded, *books)

    table = lax.all_to_all(packed, "shard", split_axis=0, concat_axis=0, tiled=True)
    best, scores = pl.pallas_call(
        functools.partial(finish_kernel, tokens, passages),
        out_shape=(
            jax.ShapeDtypeStruct((1, tokens), jnp.float32),
            jax.ShapeDtypeStruct((1, candidates.shape[2]), jnp.float32),
        ),
        in_specs=[vmem, vmem],
        out_specs=(vmem, vmem),
        compiler_params=pltpu.CompilerParams(vmem_limit_bytes=4 << 20),
    )(table, candidates[0])
    return best[None], scores[None]


def solution(mesh):
    in_specs = (
        P("rep", "shard", None, None),
        P("rep", "shard", None),
        P(("shard", "rep"), None),
        P(),
        P("shard", None),
        P("shard", None, None),
        P("shard"),
    )
    out_specs = (P("rep", "shard", None), P("rep", "shard", None))
    return jax.shard_map(on_device, mesh=mesh, in_specs=in_specs, out_specs=out_specs, check_vma=False)
```

time: 90 us -> 36.7 us (0.41)
  blocking collectives: 32.6 us -> 10.6 us
  between operations: 14.1 us -> 0.72 us
  local copies, waits for them, and re-layouts: 14.4 us -> 4.9 us
  other arithmetic: 8.9 us -> 0.01 us
  Pallas kernels: 0 us -> 5.77 us
  waiting for transfers between devices: 9.59 us -> 5.45 us
  matrix products: 1.21 us -> 0 us
    all_gather x1 -> x0, blocking collectives: 32.6 us -> none  [on_device(): lax.all_gather(queries, 'shard', axis=1, tiled=True)]
    all_to_all x0 -> x1, blocking collectives: none -> 10.6 us  [on_device(): lax.all_to_all(packed, 'shard', split_axis=0, concat_axis=0, tiled=True)]
    ppermute x0 -> x7, starting transfers between devices: none -> 8.94 us  [exchange(): return lax.ppermute(value, axis, [(i, i ^ mask) for i in range(count)])]
    all_to_all x2 -> x0, waiting for transfers between devices: 8.89 us -> none  [the longest x1 5.02 us: on_device(): lax.all_to_all(score_table, 'shard', split_axis=0, concat_axis=1, tiled=T...]
    all_to_all x2 -> x0, starting transfers between devices: 8.75 us -> none  [the longest x1 5.5 us: on_device(): lax.all_to_all(score_table, 'shard', split_axis=0, concat_axis=1, tiled=T...]
    gather x2 -> x0, local copies, waits for them, and re-layouts: 7.82 us -> none  [the longest x1 7.04 us: on_device(): jnp.take(shard_book, centroid_ids.reshape(-1), axis=0)]
    pallas_call x0 -> x3, Pallas kernels: none -> 5.77 us  [the longest x1 3.27 us: on_device(): pl.pallas_call(embed_kernel, out_shape=jax.ShapeDtypeStruct((rows, featur...]
    ppermute x0 -> x7, waiting for transfers between devices: none -> 5.45 us  [exchange(): return lax.ppermute(value, axis, [(i, i ^ mask) for i in range(count)])]
  transfers between devices with their start and end apart: 3 -> 7, of which waited for: 2 -> 3; matrix products, arithmetic and copies ran while one was open for 9% -> 2% of each run, Pallas kernels for 0% -> 0%
where the time goes in v1:
time: 36.7 us; the launch traced here: 36.3 us
  blocking collectives  10.6 us (29%)
  starting transfers between devices  8.94 us (24%)
  Pallas kernels  5.77 us (16%)
  waiting for transfers between devices  5.45 us (15%)
  local copies, waits for them, and re-layouts  4.9 us (13%)
  between operations  0.72 us (2%)
    all_to_all x1, blocking collectives, on_device(): lax.all_to_all(packed, 'shard', split_axis=0, concat_axis=0, tiled=True)  10.6 us
    ppermute x7, starting transfers between devices, exchange(): return lax.ppermute(value, axis, [(i, i ^ mask) for i in range(count)])  8.94 us
    ppermute x7, waiting for transfers between devices, exchange(): return lax.ppermute(value, axis, [(i, i ^ mask) for i in range(count)])  5.45 us
    unnamed x18, local copies, waits for them, and re-layouts  4.89 us
    pallas_call x1, Pallas kernels, on_device(): pl.pallas_call(embed_kernel, out_shape=jax.ShapeDtypeStruct((rows, featur...  3.27 us
    pallas_call x1, Pallas kernels, on_device(): pl.pallas_call(functools.partial(score_kernel, tokens), out_shape=jax.Sha...  1.72 us
    pallas_call x1, Pallas kernels, on_device(): pl.pallas_call(functools.partial(finish_kernel, tokens, passages), out_sh...  0.78 us
  transfers between devices with their start and end apart: 7, of which 3 were waited for; matrix products, arithmetic and copies ran while one was open for 2% of the time, Pallas kernels for 0%

profile of v1, /device:TPU:0, one launch (start us, length us, event | category | flops | bytes accessed | tf_op | source)
XLA Modules:
  0.0 36.3 jit_solution(15958747840612607862)
XLA Ops:
  0.6 3.0 %collective-permute-start.5 = (bf16[1024,128]{1,0:T(8,128)(2,1)}, bf16[1024,128]{1,0:T(8,128)(2,1)S(1)}, u32[]{:S(2)}, u32[]{:S(2)}) collective-permute-start(bf16[1024,128]{1,0:T(8,128)(2,1)} %refs_0_.3), channel_id=1, source_target_pairs={{0,2},{1,3},{2,0},{3,1},{4,6},{5,7},{6,4},{7,5},{8,10},{9,11},{10,... | collective-permute-start | bytes 786440 | tf_op jit(solution)/shard_map/ppermute | solution.py:18
  3.7 0.0 collective-permute-start.4
  3.7 1.5 %collective-permute-start = (bf16[1,32,128]{2,1,0:T(8,128)(2,1)}, bf16[1,32,128]{2,1,0:T(8,128)(2,1)S(1)}, u32[]{:S(2)}, u32[]{:S(2)}) collective-permute-start(bf16[1,32,128]{2,1,0:T(8,128)(2,1)} %bitcast.16), channel_id=1, source_target_pairs={{0,4},{4,0},{8,12},{12,8},{16,20},{20,16},{24,28},{28,24},{1,5},{5... | collective-permute-start | bytes 24584 | tf_op jit(solution)/shard_map/ppermute | solution.py:18
  5.2 0.7 %constant_dynamic-update-slice_fusion.4 = bf16[8,32,128]{2,1,0:T(8,128)(2,1)S(1)} fusion(bf16[1,1,32,128]{3,2,1,0:T(8,128)(2,1)} %param.7), kind=kLoop, calls=%fused_computation.5 | loop fusion | bytes 16384
  5.9 0.0 copy-start.6
  5.9 1.6 %collective-permute-done = bf16[1,32,128]{2,1,0:T(8,128)(2,1)S(1)} collective-permute-done((bf16[1,32,128]{2,1,0:T(8,128)(2,1)}, bf16[1,32,128]{2,1,0:T(8,128)(2,1)S(1)}, u32[]{:S(2)}, u32[]{:S(2)}) %collective-permute-start) | collective-permute-done | bytes 8224 | tf_op jit(solution)/shard_map/ppermute | solution.py:18
  7.5 0.0 copy-done.6
  7.5 3.6 %collective-permute-start.3 = (bf16[2,32,128]{2,1,0:T(8,128)(2,1)S(1)}, bf16[2,32,128]{2,1,0:T(8,128)(2,1)S(1)}, u32[]{:S(2)}, u32[]{:S(2)}) collective-permute-start(bf16[2,32,128]{2,1,0:T(8,128)(2,1)S(1)} %pad_maximum_fusion), channel_id=1, source_target_pairs={{0,24},{4,28},{8,16},{12,20},{16,8},{20,12},{24,0},{28,4},{1,25},{... | collective-permute-start | bytes 49160 | tf_op jit(solution)/shard_map/ppermute | solution.py:18
  11.1 0.0 collective-permute-start.2
  11.1 0.8 %collective-permute-start.1 = (bf16[2,32,128]{2,1,0:T(8,128)(2,1)S(1)}, bf16[2,32,128]{2,1,0:T(8,128)(2,1)S(1)}, u32[]{:S(2)}, u32[]{:S(2)}) collective-permute-start(bf16[2,32,128]{2,1,0:T(8,128)(2,1)S(1)} %pad_maximum_fusion), channel_id=1, source_target_pairs={{0,8},{4,12},{8,0},{12,4},{16,24},{20,28},{24,16},{28,20},{1,9},{5... | collective-permute-start | bytes 49160 | tf_op jit(solution)/shard_map/ppermute | solution.py:18
  11.9 0.0 collective-permute-done.5.refs_2_
  11.9 0.0 collective-permute-start.6
  11.9 2.9 %collective-permute-done.1 = bf16[2,32,128]{2,1,0:T(8,128)(2,1)S(1)} collective-permute-done((bf16[2,32,128]{2,1,0:T(8,128)(2,1)S(1)}, bf16[2,32,128]{2,1,0:T(8,128)(2,1)S(1)}, u32[]{:S(2)}, u32[]{:S(2)}) %collective-permute-start.1) | collective-permute-done | bytes 16416 | tf_op jit(solution)/shard_map/ppermute | solution.py:18
  14.9 0.9 %collective-permute-done.2 = bf16[2,32,128]{2,1,0:T(8,128)(2,1)S(1)} collective-permute-done((bf16[2,32,128]{2,1,0:T(8,128)(2,1)S(1)}, bf16[2,32,128]{2,1,0:T(8,128)(2,1)S(1)}, u32[]{:S(2)}, u32[]{:S(2)}) %collective-permute-start.2) | collective-permute-done | bytes 16416 | tf_op jit(solution)/shard_map/ppermute | solution.py:18
  15.8 0.0 collective-permute-done.3
  15.8 0.0 copy-start.5
  15.8 0.0 collective-permute-done.4.refs_1_
  15.8 0.0 collective-permute-done.6.refs_3_
  15.8 0.6 %copy-done.4 = s32[16,128]{1,0:T(8,128)S(1)} copy-done((s32[16,128]{1,0:T(8,128)S(1)}, s32[16,128]{1,0:T(8,128)}, u32[]{:S(2)}) %copy-start.4) | copy-done | bytes 8216
  16.5 0.0 copy-done.5
  16.5 0.0 copy-start
  16.5 0.9 %copy-done = bf16[1024,128]{1,0:T(8,128)(2,1)S(1)} copy-done((bf16[1024,128]{1,0:T(8,128)(2,1)S(1)}, bf16[1024,128]{1,0:T(8,128)(2,1)}, u32[]{:S(2)}) %copy-start) | copy-done | bytes 262168
  17.4 0.0 copy-start.3
  17.4 1.2 %copy-done.3 = s32[16,128,128]{2,1,0:T(8,128)S(1)} copy-done((s32[16,128,128]{2,1,0:T(8,128)S(1)}, s32[16,128,128]{2,1,0:T(8,128)}, u32[]{:S(2)}) %copy-start.3) | copy-done | bytes 1048600
  18.7 3.3 %shard_map.86.embedded_ref = bf16[2048,128]{1,0:T(8,128)(2,1)S(1)} custom-call(s32[1]{0:T(128)} %bitcast.3.rep_ref, f32[4]{0:T(128)S(1)} %copy-done.5, s32[16,128]{1,0:T(8,128)S(1)} %copy-done.4, s32[16,128,128]{2,1,0:T(8,128)S(1)} %copy-done.3, bf16[1024,128]{1,0:T(8,128)(2,1)S(1)} %copy-done, bf16[1024,128]{1,0:T(8,128)(2,1)S(1)} %collective-permute-done.4.refs_1_, ...), custom_call_target="tpu_custom_call" | custom-call | flops 2147483648 | bytes 2097152 | tf_op jit(solution)/shard_map/pallas_call | solution.py:154
  21.9 0.0 copy-start.1
  21.9 0.6 %copy-done.1 = s32[16]{0:T(128)S(1)} copy-done((s32[16]{0:T(128)S(1)}, s32[16]{0:T(128)}, u32[]{:S(2)}) %copy-start.1) | copy-done | bytes 88
  22.6 1.7 %shard_map.87 = f32[8,128]{1,0:T(8,128)S(1)} custom-call(s32[1]{0:T(128)} %bitcast.shard_ref, s32[16]{0:T(128)S(1)} %copy-done.1, bf16[256,128]{1,0:T(8,128)(2,1)S(1)} %bitcast.12, bf16[2048,128]{1,0:T(8,128)(2,1)S(1)} %shard_map.86.embedded_ref, bf16[1024,128]{1,0:T(8,128)(2,1)S(1)} %copy-done, bf16[1024,128]{1,0:T(8,128)(2,1)S(1)} %collective-permute-done.4.refs_1_, ...), custom_call_target="tpu_custom_call" | custom-call | flops 402653184 | bytes 2097152 | tf_op jit(solution)/shard_map/pallas_call | solution.py:170
  24.3 10.6 %all_to_all.11 = f32[8,1,128]{2,1,0:T(1,128)S(1)} all-to-all(f32[8,1,128]{2,1,0:T(1,128)S(1)} %bitcast.13), channel_id=1, replica_groups=mesh['shard'=8,'rep'=4] {'shard'}, dimensions={0} | all-to-all | bytes 8192 | tf_op jit(solution)/shard_map/all_to_all | solution.py:180
  34.9 0.0 copy-start.2
  34.9 0.7 %copy-done.2 = s32[1,1,64]{2,1,0:T(1,128)S(1)} copy-done((s32[1,1,64]{2,1,0:T(1,128)S(1)}, s32[1,1,64]{2,1,0:T(1,128)}, u32[]{:S(2)}) %copy-start.2) | copy-done | bytes 280
  35.6 0.8 %shard_map.88 = (f32[1,32]{1,0:T(1,128)}, f32[1,64]{1,0:T(1,128)}) custom-call(f32[8,128]{1,0:T(8,128)S(1)} %bitcast.14, s32[1,64]{1,0:T(1,128)S(1)} %bitcast.15), custom_call_target="tpu_custom_call" | custom-call | tf_op jit(solution)/shard_map/pallas_call | solution.py:181
  (6 shorter events, 0.0 us)
Async XLA Ops:
  0.6 11.3 %collective-permute-start.5 = (bf16[1024,128]{1,0:T(8,128)(2,1)}, bf16[1024,128]{1,0:T(8,128)(2,1)S(1)}, u32[]{:S(2)}, u32[]{:S(2)}) collective-permute-start(bf16[1024,128]{1,0:T(8,128)(2,1)} %refs_0_.3), channel_id=1, source_target_pairs={{0,2},{1,3},{2,0},{3,1},{4,6},{5,7},{6,4},{7,5},{8,10},{9,11},{10,... | collective-permute-start | bytes 786440 | tf_op jit(solution)/shard_map/ppermute | solution.py:18
  3.7 12.2 %collective-permute-start.4 = (bf16[1024,128]{1,0:T(8,128)(2,1)}, bf16[1024,128]{1,0:T(8,128)(2,1)S(1)}, u32[]{:S(2)}, u32[]{:S(2)}) collective-permute-start(bf16[1024,128]{1,0:T(8,128)(2,1)} %refs_0_.3), channel_id=1, source_target_pairs={{0,1},{1,0},{2,3},{3,2},{4,5},{5,4},{6,7},{7,6},{8,9},{9,8},{10,11... | collective-permute-start | bytes 786440 | tf_op jit(solution)/shard_map/ppermute | solution.py:18
  3.7 3.9 %collective-permute-start = (bf16[1,32,128]{2,1,0:T(8,128)(2,1)}, bf16[1,32,128]{2,1,0:T(8,128)(2,1)S(1)}, u32[]{:S(2)}, u32[]{:S(2)}) collective-permute-start(bf16[1,32,128]{2,1,0:T(8,128)(2,1)} %bitcast.16), channel_id=1, source_target_pairs={{0,4},{4,0},{8,12},{12,8},{16,20},{20,16},{24,28},{28,24},{1,5},{5... | collective-permute-start | bytes 24584 | tf_op jit(solution)/shard_map/ppermute | solution.py:18
  5.9 1.6 %copy-start.6 = (bf16[1,1,32,128]{3,2,1,0:T(8,128)(2,1)S(1)}, bf16[1,1,32,128]{3,2,1,0:T(8,128)(2,1)}, u32[]{:S(2)}) copy-start(bf16[1,1,32,128]{3,2,1,0:T(8,128)(2,1)} %param.7) | copy-start | bytes 24580
  7.5 8.3 %collective-permute-start.3 = (bf16[2,32,128]{2,1,0:T(8,128)(2,1)S(1)}, bf16[2,32,128]{2,1,0:T(8,128)(2,1)S(1)}, u32[]{:S(2)}, u32[]{:S(2)}) collective-permute-start(bf16[2,32,128]{2,1,0:T(8,128)(2,1)S(1)} %pad_maximum_fusion), channel_id=1, source_target_pairs={{0,24},{4,28},{8,16},{12,20},{16,8},{20,12},{24,0},{28,4},{1,25},{... | collective-permute-start | bytes 49160 | tf_op jit(solution)/shard_map/ppermute | solution.py:18
  11.1 4.6 %collective-permute-start.2 = (bf16[2,32,128]{2,1,0:T(8,128)(2,1)S(1)}, bf16[2,32,128]{2,1,0:T(8,128)(2,1)S(1)}, u32[]{:S(2)}, u32[]{:S(2)}) collective-permute-start(bf16[2,32,128]{2,1,0:T(8,128)(2,1)S(1)} %pad_maximum_fusion), channel_id=1, source_target_pairs={{0,16},{4,20},{8,24},{12,28},{16,0},{20,4},{24,8},{28,12},{1,17},{... | collective-permute-start | bytes 49160 | tf_op jit(solution)/shard_map/ppermute | solution.py:18
  11.1 3.7 %collective-permute-start.1 = (bf16[2,32,128]{2,1,0:T(8,128)(2,1)S(1)}, bf16[2,32,128]{2,1,0:T(8,128)(2,1)S(1)}, u32[]{:S(2)}, u32[]{:S(2)}) collective-permute-start(bf16[2,32,128]{2,1,0:T(8,128)(2,1)S(1)} %pad_maximum_fusion), channel_id=1, source_target_pairs={{0,8},{4,12},{8,0},{12,4},{16,24},{20,28},{24,16},{28,20},{1,9},{5... | collective-permute-start | bytes 49160 | tf_op jit(solution)/shard_map/ppermute | solution.py:18
  11.9 3.9 %collective-permute-start.6 = (bf16[1024,128]{1,0:T(8,128)(2,1)S(1)}, bf16[1024,128]{1,0:T(8,128)(2,1)S(1)}, u32[]{:S(2)}, u32[]{:S(2)}) collective-permute-start(bf16[1024,128]{1,0:T(8,128)(2,1)S(1)} %collective-permute-done.5.refs_2_), channel_id=1, source_target_pairs={{0,1},{1,0},{2,3},{3,2},{4,5},{5,4},{6,7},{7,6},{8,9},{9,8},{10,11... | collective-permute-start | bytes 786440 | tf_op jit(solution)/shard_map/ppermute | solution.py:18
  15.8 0.7 %copy-start.4 = (s32[16,128]{1,0:T(8,128)S(1)}, s32[16,128]{1,0:T(8,128)}, u32[]{:S(2)}) copy-start(s32[16,128]{1,0:T(8,128)} %ids_ref.1) | copy-start | bytes 24580
  15.8 0.7 %copy-start.5 = (f32[4]{0:T(128)S(1)}, f32[4]{0:T(128)}, u32[]{:S(2)}) copy-start(f32[4]{0:T(128)} %weight_ref.1) | copy-start | bytes 52
  16.5 1.0 %copy-start = (bf16[1024,128]{1,0:T(8,128)(2,1)S(1)}, bf16[1024,128]{1,0:T(8,128)(2,1)}, u32[]{:S(2)}) copy-start(bf16[1024,128]{1,0:T(8,128)(2,1)} %refs_0_.3) | copy-start | bytes 786436
  17.4 1.2 %copy-start.3 = (s32[16,128,128]{2,1,0:T(8,128)S(1)}, s32[16,128,128]{2,1,0:T(8,128)}, u32[]{:S(2)}) copy-start(s32[16,128,128]{2,1,0:T(8,128)} %codes_ref.1) | copy-start | bytes 3145732
  21.9 0.7 %copy-start.1 = (s32[16]{0:T(128)S(1)}, s32[16]{0:T(128)}, u32[]{:S(2)}) copy-start(s32[16]{0:T(128)} %length_ref.1) | copy-start | bytes 196
  34.9 0.7 %copy-start.2 = (s32[1,1,64]{2,1,0:T(1,128)S(1)}, s32[1,1,64]{2,1,0:T(1,128)}, u32[]{:S(2)}) copy-start(s32[1,1,64]{2,1,0:T(1,128)} %param.8) | copy-start | bytes 772

commit v2 on v1

v2 whole, which is shorter than its diff:
```python
import functools

import jax
import jax.numpy as jnp
from jax import lax
from jax.experimental import pallas as pl
from jax.experimental.pallas import tpu as pltpu
from jax.sharding import PartitionSpec as P


FAR_BELOW = -1e30
LANES = 128
LOW = 256
BOOK_CHUNK = 128
EXACT = lax.Precision.HIGHEST


def exchange(value, axis, mask):
    count = lax.axis_size(axis)
    return lax.ppermute(value, axis, [(i, i ^ mask) for i in range(count)])


def gather_by_xor(block, axis):
    count = lax.axis_size(axis)
    held = block[None]
    reach = 2
    while reach < count:
        step = 2 if reach * 2 == count else 4
        parts = []
        for k in range(step - 1, 0, -1):
            parts.insert(0, exchange(held, axis, reach * k))
        held = jnp.concatenate([held] + parts, axis=0)
        reach *= step
    if count == 1:
        return [held]
    return [held, exchange(held, axis, 1)]


def owner_mask(place, count):
    half = max(1, count // 2)
    return (place % half) * 2 + place // half


def named_rows(total, onehot, high, book_ref, first):
    for j in range(0, book_ref.shape[0] // LOW, 2):
        pair = jnp.concatenate(
            [book_ref[(j + h) * LOW : (j + h + 1) * LOW, :] for h in range(2)], axis=1
        )
        found = jnp.dot(onehot, pair, preferred_element_type=jnp.float32)
        for h in range(2):
            total = jnp.where(high == first + (j + h), found[:, h * LANES : (h + 1) * LANES], total)
    return total


def first_of(k, book_ref):
    return (lax.axis_index("rep") ^ k) * (book_ref.shape[0] // LOW)


def prepare_kernel(
    tokens, ids_hbm, own_hbm, length_hbm, cands_hbm,
    onehot_ref, high_ref, sum_ref, live_ref, mine_ref, owner_ref, column_ref,
    ids_ref, own_ref, length_ref, cands_ref, sems
):
    sources, places = (ids_hbm, own_hbm, length_hbm, cands_hbm), (ids_ref, own_ref, length_ref, cands_ref)
    copies = [pltpu.make_async_copy(*pair, sems.at[i]) for i, pair in enumerate(zip(sources, places))]
    for copy in copies:
        copy.start()
    passages, slots = ids_ref.shape
    shape = mine_ref.shape
    shard = lax.axis_index("shard")
    mask = owner_mask(lax.broadcasted_iota(jnp.int32, shape, 1) // tokens, shape[0])
    mine_ref[...] = ((lax.broadcasted_iota(jnp.int32, shape, 0) ^ shard) == mask).astype(jnp.float32)
    copies[0].wait()
    ids_by_slot = jnp.transpose(ids_ref[...])
    lane = lax.broadcasted_iota(jnp.int32, (slots, LANES), 1)
    first = first_of(0, own_ref)
    for p in range(passages):
        here = pl.ds(p * slots, slots)
        ids = jnp.broadcast_to(ids_by_slot[:, p : p + 1], (slots, LANES))
        low = ids & (LOW - 1)
        onehot_ref[here, :] = jnp.concatenate(
            [(low == lane + k * LANES).astype(jnp.float32) for k in range(LOW // LANES)], axis=1
        ).astype(jnp.bfloat16)
        high_ref[here, :] = ids >> (LOW.bit_length() - 1)
    for copy in copies[1:]:
        copy.wait()
    for p in range(passages):
        live_ref[p : p + 1, :] = jnp.broadcast_to(length_ref[:, p : p + 1], (1, live_ref.shape[1]))
    cands = cands_ref[...]
    owner_ref[...] = (
        lax.broadcasted_iota(jnp.int32, owner_ref.shape, 0) == cands // passages
    ).astype(jnp.float32)
    column_ref[...] = tokens + cands % passages
    for p in range(passages):
        here = pl.ds(p * slots, slots)
        zeros = jnp.zeros((slots, LANES), jnp.float32)
        sum_ref[here, :] = named_rows(zeros, onehot_ref[here, :], high_ref[here, :], own_ref, first)


def fold_kernel(blocks, weight_hbm, codes_hbm, onehot_ref, high_ref, sum_ref, *refs):
    *book_refs, out_ref, residual_ref, weight_ref, codes_ref, sems = refs
    copies = (
        pltpu.make_async_copy(weight_hbm, weight_ref, sems.at[0]),
        pltpu.make_async_copy(codes_hbm, codes_ref, sems.at[1]),
    )
    for copy in copies:
        copy.start()
    passages, slots, _ = codes_ref.shape
    for p in range(passages):
        here = pl.ds(p * slots, slots)
        total = sum_ref[here, :]
        for k, book_ref in zip(blocks, book_refs):
            total = named_rows(total, onehot_ref[here, :], high_ref[here, :], book_ref, first_of(k, book_ref))
        out_ref[here, :] = total
    for copy in copies:
        copy.wait()
    levels = weight_ref.shape[1]
    values = [jnp.broadcast_to(weight_ref[:, k : k + 1], (slots, LANES)) for k in range(levels)]
    for p in range(passages):
        codes = codes_ref[p]
        residual = values[levels - 1]
        for level in range(levels - 2, -1, -1):
            residual = jnp.where(codes == level, values[level], residual)
        residual_ref[pl.ds(p * slots, slots), :] = residual


def score_kernel(
    tokens, parts, live_ref, mine_ref, onehot_ref, high_ref, residual_ref, sum_ref, *refs, last
):
    *book_refs, out_ref, embedded_ref = refs[parts:]
    passages = live_ref.shape[0]
    slots = residual_ref.shape[0] // passages
    queries = jnp.concatenate([ref[...] for ref in refs[:parts]], axis=0)
    width = queries.shape[0]

    def product(rows):
        return lax.dot_general(
            rows, queries, (((1,), (1,)), ((), ())), preferred_element_type=jnp.float32
        )

    best = jnp.full((8, width), FAR_BELOW, jnp.float32)
    for book_ref in book_refs:
        chunk = min(BOOK_CHUNK, book_ref.shape[0])
        for c in range(book_ref.shape[0] // chunk):
            found = product(book_ref[c * chunk : (c + 1) * chunk, :])
            best = jnp.maximum(best, jnp.max(found.reshape(chunk // 8, 8, width), axis=0))
    slot = lax.broadcasted_iota(jnp.int32, (slots, width), 0)
    tops = []
    for p in range(passages):
        here = pl.ds(p * slots, slots)
        total = sum_ref[here, :]
        for k in last:
            total = named_rows(total, onehot_ref[here, :], high_ref[here, :], book_refs[k], first_of(k, book_refs[k]))
        embedded_ref[here, :] = (total + residual_ref[here, :]).astype(jnp.bfloat16)
    for p in range(passages):
        here = pl.ds(p * slots, slots)
        found = jnp.where(slot < live_ref[p : p + 1, :], product(embedded_ref[here, :]), FAR_BELOW)
        tops.append(jnp.max(found, axis=0, keepdims=True))
    best = jnp.max(best, axis=0, keepdims=True)
    room = out_ref.shape[1]
    table = jnp.concatenate(
        [jnp.zeros((tokens, width), jnp.float32)]
        + tops
        + [jnp.zeros((room - tokens - passages, width), jnp.float32)],
        axis=0,
    )
    mine = mine_ref[...]
    sums = lax.dot_general(
        mine, table, (((1,), (1,)), ((), ())), preferred_element_type=jnp.float32, precision=EXACT
    )
    kept = mine * best
    while kept.shape[1] > LANES:
        half = kept.shape[1] // 2
        kept = kept[:, :half] + kept[:, half:]
    shift = LANES // 2
    while shift >= tokens:
        kept = kept + pltpu.roll(kept, shift, 1)
        shift //= 2
    where = lax.broadcasted_iota(jnp.int32, kept.shape, 1)
    rows = jnp.where(where < tokens, kept, sums)
    out_ref[...] = jnp.where(pl.program_id(0) == 0, rows, out_ref[...] + rows)


def finish_kernel(tokens, table_ref, owner_ref, column_ref, best_ref, scores_ref):
    table = table_ref[...]
    best_ref[...] = jnp.max(table, axis=0, keepdims=True)[:, 0:tokens]
    columns = lax.dot_general(
        table, owner_ref[...], (((0,), (0,)), ((), ())), preferred_element_type=jnp.float32, precision=EXACT
    )
    wanted = lax.broadcasted_iota(jnp.int32, columns.shape, 0) == column_ref[...]
    scores_ref[...] = jnp.sum(jnp.where(wanted, columns, 0.0), axis=0, keepdims=True)


def on_device(queries, candidates, codebook, bucket_weights, centroid_ids, residual_codes, passage_lengths):
    tokens, features = queries.shape[2:]
    passages, slots = centroid_ids.shape
    wanted = candidates.shape[2]
    shards, reps = lax.axis_size("shard"), lax.axis_size("rep")
    vmem = pl.BlockSpec(memory_space=pltpu.VMEM)
    rows = passages * slots
    width = min(256, shards * tokens)
    room = LANES

    books = {0: codebook}
    bit = reps // 2
    while bit:
        for k in list(books):
            books[k ^ bit] = exchange(books[k], "rep", bit)
        bit //= 2
    last = (reps - 1,) if reps > 1 else ()
    middle = tuple(k for k in range(1, reps) if k not in last)

    def shaped(*shape, dtype=jnp.float32):
        return jax.ShapeDtypeStruct(shape, dtype)

    def kernel(body, limit=24, **more):
        return pl.pallas_call(
            body,
            compiler_params=pltpu.CompilerParams(vmem_limit_bytes=limit << 20),
            cost_estimate=pl.CostEstimate(flops=1 << 30, bytes_accessed=2 << 20, transcendentals=0),
            **more,
        )

    hbm = pl.BlockSpec(memory_space=pltpu.HBM)

    def in_hbm(value):
        return pltpu.with_memory_space_constraint(value, pltpu.HBM)

    onehot, high, total, live, mine, owner, column = kernel(
        functools.partial(prepare_kernel, tokens),
        out_shape=(
            shaped(rows, LOW, dtype=jnp.bfloat16),
            shaped(rows, LANES, dtype=jnp.int32),
            shaped(rows, features),
            shaped(passages, width, dtype=jnp.int32),
            shaped(shards, shards * tokens),
            shaped(shards, wanted),
            shaped(1, wanted, dtype=jnp.int32),
        ),
        in_specs=[hbm] * 4,
        out_specs=(vmem,) * 7,
        scratch_shapes=[
            pltpu.VMEM(centroid_ids.shape, jnp.int32),
            pltpu.VMEM(codebook.shape, codebook.dtype),
            pltpu.VMEM((1, passages), jnp.int32),
            pltpu.VMEM((1, wanted), jnp.int32),
            pltpu.SemaphoreType.DMA((4,)),
        ],
    )(*map(in_hbm, (centroid_ids, codebook, passage_lengths.reshape(1, passages), candidates[0])))
    groups = [part.reshape(-1, features) for part in gather_by_xor(queries[0, 0], "shard")]
    if shards * tokens > width:
        groups = [jnp.concatenate(groups, axis=0)]
    total, residual = kernel(
        functools.partial(fold_kernel, middle),
        out_shape=(shaped(rows, features), shaped(rows, features)),
        in_specs=[hbm, hbm] + [vmem] * (3 + len(middle)),
        out_specs=(vmem, vmem),
        scratch_shapes=[
            pltpu.VMEM((1, bucket_weights.shape[0]), jnp.float32),
            pltpu.VMEM(residual_codes.shape, jnp.int32),
            pltpu.SemaphoreType.DMA((2,)),
        ],
    )(in_hbm(bucket_weights.reshape(1, -1)), in_hbm(residual_codes), onehot, high, total, *[books[k] for k in middle])

    packed = kernel(
        functools.partial(score_kernel, tokens, len(groups), last=last),
        out_shape=shaped(shards, room),
        grid=(shards * tokens // width,),
        in_specs=[vmem, pl.BlockSpec((shards, width), lambda i: (0, i))]
        + [vmem] * 4
        + [pl.BlockSpec((width // len(groups), features), lambda i: (i, 0))] * len(groups)
        + [vmem] * reps,
        out_specs=vmem,
        scratch_shapes=[pltpu.VMEM((rows, features), jnp.bfloat16)],
    )(live, mine, onehot, high, residual, total, *groups, *[books[k] for k in range(reps)])

    table = lax.all_to_all(packed, "shard", split_axis=0, concat_axis=0, tiled=True)
    best, scores = pl.pallas_call(
        functools.partial(finish_kernel, tokens),
        out_shape=(shaped(1, tokens), shaped(1, wanted)),
        in_specs=[vmem] * 3,
        out_specs=(vmem, vmem),
        compiler_params=pltpu.CompilerParams(vmem_limit_bytes=4 << 20),
    )(table, owner, column)
    return best[None], scores[None]


def solution(mesh):
    in_specs = (
        P("rep", "shard", None, None),
        P("rep", "shard", None),
        P(("shard", "rep"), None),
        P(),
        P("shard", None),
        P("shard", None, None),
        P("shard"),
    )
    out_specs = (P("rep", "shard", None), P("rep", "shard", None))

    return jax.shard_map(on_device, mesh=mesh, in_specs=in_specs, out_specs=out_specs, check_vma=False)
```

time: 36.7 us -> 31.5 us (0.86)
  local copies, waits for them, and re-layouts: 4.9 us -> 0.01 us
  waiting for transfers between devices: 5.45 us -> 4.08 us
  Pallas kernels: 5.77 us -> 6.43 us
  blocking collectives: 10.6 us -> 11.1 us
    unnamed x18 -> x4, local copies, waits for them, and re-layouts: 4.89 us -> 0.01 us
    ppermute x7, waiting for transfers between devices: 5.45 us -> 4.08 us  [exchange(): return lax.ppermute(value, axis, [(i, i ^ mask) for i in range(count)])]
    pallas_call x3 -> x4, Pallas kernels: 5.77 us -> 6.43 us  [the longest x1 1.96 us: on_device(): kernel(functools.partial(prepare_kernel, tokens), out_shape=(shaped(rows,...]
    all_to_all x1, blocking collectives: 10.6 us -> 11.1 us  [on_device(): lax.all_to_all(packed, 'shard', split_axis=0, concat_axis=0, tiled=True)]
  transfers between devices with their start and end apart: 7 -> 7, of which waited for: 3 -> 3; matrix products, arithmetic and copies ran while one was open for 2% -> 0% of each run, Pallas kernels for 0% -> 12%
where the time goes in v2:
time: 31.5 us; the launch traced here: 31.3 us
  blocking collectives  11.1 us (35%)
  starting transfers between devices  9.01 us (29%)
  Pallas kernels  6.43 us (20%)
  waiting for transfers between devices  4.08 us (13%)
  between operations  0.68 us (2%)
    all_to_all x1, blocking collectives, on_device(): lax.all_to_all(packed, 'shard', split_axis=0, concat_axis=0, tiled=True)  11.1 us
    ppermute x7, starting transfers between devices, exchange(): return lax.ppermute(value, axis, [(i, i ^ mask) for i in range(count)])  9.01 us
    ppermute x7, waiting for transfers between devices, exchange(): return lax.ppermute(value, axis, [(i, i ^ mask) for i in range(count)])  4.08 us
    pallas_call x1, Pallas kernels, on_device(): kernel(functools.partial(prepare_kernel, tokens), out_shape=(shaped(rows,...  1.96 us
    pallas_call x1, Pallas kernels, on_device(): kernel(functools.partial(score_kernel, tokens, len(groups), last=last), o...  1.93 us
    pallas_call x1, Pallas kernels, on_device(): kernel(functools.partial(fold_kernel, middle), out_shape=(shaped(rows, fe...  1.76 us
    pallas_call x1, Pallas kernels, on_device(): pl.pallas_call(functools.partial(finish_kernel, tokens), out_shape=(shape...  0.78 us
  transfers between devices with their start and end apart: 7, of which 3 were waited for; matrix products, arithmetic and copies ran while one was open for 0% of the time, Pallas kernels for 12%

profile of v2, /device:TPU:0, one launch (start us, length us, event | category | flops | bytes accessed | tf_op | source)
XLA Modules:
  0.0 31.3 jit_solution(7856361350785518181)
XLA Ops:
  0.6 3.0 %collective-permute-start.1 = (bf16[1024,128]{1,0:T(8,128)(2,1)}, bf16[1024,128]{1,0:T(8,128)(2,1)S(1)}, u32[]{:S(2)}, u32[]{:S(2)}) collective-permute-start(bf16[1024,128]{1,0:T(8,128)(2,1)} %refs_2_.1), channel_id=1, source_target_pairs={{0,2},{1,3},{2,0},{3,1},{4,6},{5,7},{6,4},{7,5},{8,10},{9,11},{10,... | collective-permute-start | bytes 786440 | tf_op jit(solution)/shard_map/ppermute | solution.py:20
  3.7 0.0 collective-permute-start
  3.7 1.6 %collective-permute-start.2 = (bf16[1,32,128]{2,1,0:T(8,128)(2,1)}, bf16[1,32,128]{2,1,0:T(8,128)(2,1)S(1)}, u32[]{:S(2)}, u32[]{:S(2)}) collective-permute-start(bf16[1,32,128]{2,1,0:T(8,128)(2,1)} %bitcast.16), channel_id=1, source_target_pairs={{0,8},{4,12},{8,0},{12,4},{16,24},{20,28},{24,16},{28,20},{1,9},{5... | collective-permute-start | bytes 24584 | tf_op jit(solution)/shard_map/ppermute | solution.py:20
  5.2 2.6 %collective-permute-start.3 = (bf16[1,32,128]{2,1,0:T(8,128)(2,1)}, bf16[1,32,128]{2,1,0:T(8,128)(2,1)S(1)}, u32[]{:S(2)}, u32[]{:S(2)}) collective-permute-start(bf16[1,32,128]{2,1,0:T(8,128)(2,1)} %bitcast.17), channel_id=1, source_target_pairs={{0,16},{4,20},{8,24},{12,28},{16,0},{20,4},{24,8},{28,12},{1,17},{... | collective-permute-start | bytes 24584 | tf_op jit(solution)/shard_map/ppermute | solution.py:20
  7.8 0.2 collective-permute-start.4
  8.1 2.1 %collective-permute-done.1.refs_1_.refs_4_ = bf16[1024,128]{1,0:T(8,128)(2,1)S(1)} collective-permute-done((bf16[1024,128]{1,0:T(8,128)(2,1)}, bf16[1024,128]{1,0:T(8,128)(2,1)S(1)}, u32[]{:S(2)}, u32[]{:S(2)}) %collective-permute-start.1) | collective-permute-done | bytes 262176 | tf_op jit(solution)/shard_map/ppermute | solution.py:20
  10.2 0.0 collective-permute-start.6
  10.2 0.0 copy-start.1
  10.2 2.0 %shard_map.86 = (bf16[2048,256]{1,0:T(8,128)(2,1)S(1)}, s32[2048,128]{1,0:T(8,128)S(1)}, f32[2048,128]{1,0:T(8,128)S(1)}, s32[16,256]{1,0:T(8,128)S(1)}, f32[8,2...) custom-call(s32[16,128]{1,0:T(8,128)} %ids_hbm.1, bf16[1024,128]{1,0:T(8,128)(2,1)} %refs_2_.1, ...), custom_call_target="tpu_custom_call" | custom-call | flops 1073741824 | bytes 2097152 | tf_op jit(solution)/shard_map/pallas_call | solution.py:229
  12.2 0.0 collective-permute-done.2
  12.2 0.0 collective-permute-done.3
  12.2 1.3 %collective-permute-done.4 = bf16[1,32,128]{2,1,0:T(8,128)(2,1)S(1)} collective-permute-done((bf16[1,32,128]{2,1,0:T(8,128)(2,1)}, bf16[1,32,128]{2,1,0:T(8,128)(2,1)S(1)}, u32[]{:S(2)}, u32[]{:S(2)}) %collective-permute-start.4) | collective-permute-done | bytes 8224 | tf_op jit(solution)/shard_map/ppermute | solution.py:20
  13.5 0.0 copy-done.1
  13.5 1.6 %collective-permute-start.5 = (bf16[4,32,128]{2,1,0:T(8,128)(2,1)S(1)}, bf16[4,32,128]{2,1,0:T(8,128)(2,1)S(1)}, u32[]{:S(2)}, u32[]{:S(2)}) collective-permute-start(bf16[4,32,128]{2,1,0:T(8,128)(2,1)S(1)} %pad_maximum_fusion), channel_id=1, source_target_pairs={{0,4},{4,0},{8,12},{12,8},{16,20},{20,16},{24,28},{28,24},{1,5},{5... | collective-permute-start | bytes 98312 | tf_op jit(solution)/shard_map/ppermute | solution.py:20
  15.1 0.0 collective-permute-done.refs_0_.refs_3_
  15.1 0.0 copy-start
  15.1 1.8 %shard_map.87 = (f32[2048,128]{1,0:T(8,128)S(1)}, f32[2048,128]{1,0:T(8,128)S(1)}) custom-call(f32[1,4]{1,0:T(1,128)} %bitcast.20, s32[16,128,128]{2,1,0:T(8,128)} %codes_hbm.1, bf16[2048,256]{1,0:T(8,128)(2,1)S(1)} %get-tuple-element.15.onehot_ref, s32[2048,128]{1,0:T(8,128)S(1)} %get-tuple-element.16.high_ref, f32[2048,128]{1,0:T(8,128)S(1)} %get-tuple-element.17.sum_ref, ...), custom_call_target="tpu_custom_call" | custom-call | flops 1073741824 | bytes 2097152 | tf_op jit(solution)/shard_map/pallas_call | solution.py:253
  16.9 0.6 %collective-permute-done.5 = bf16[4,32,128]{2,1,0:T(8,128)(2,1)S(1)} collective-permute-done((bf16[4,32,128]{2,1,0:T(8,128)(2,1)S(1)}, bf16[4,32,128]{2,1,0:T(8,128)(2,1)S(1)}, u32[]{:S(2)}, u32[]{:S(2)}) %collective-permute-start.5) | collective-permute-done | bytes 32800 | tf_op jit(solution)/shard_map/ppermute | solution.py:20
  17.5 0.0 collective-permute-done.6.refs_5_
  17.5 0.0 copy-done
  17.5 1.9 %shard_map.88 = f32[8,128]{1,0:T(8,128)S(1)} custom-call(s32[16,256]{1,0:T(8,128)S(1)} %get-tuple-element.13.live_ref, f32[8,256]{1,0:T(8,128)S(1)} %get-tuple-element.14.mine_ref, bf16[2048,256]{1,0:T(8,128)(2,1)S(1)} %get-tuple-element.15.onehot_ref, s32[2048,128]{1,0:T(8,128)S(1)} %get-tuple-element.16.high_ref, ...), custom_call_target="tpu_custom_call" | custom-call | flops 1073741824 | bytes 2097152 | tf_op jit(solution)/shard_map/pallas_call | solution.py:265
  19.4 11.1 %all_to_all.11 = f32[8,1,128]{2,1,0:T(1,128)S(1)} all-to-all(f32[8,1,128]{2,1,0:T(1,128)S(1)} %bitcast.14), channel_id=1, replica_groups=mesh['shard'=8,'rep'=4] {'shard'}, dimensions={0} | all-to-all | bytes 8192 | tf_op jit(solution)/shard_map/all_to_all | solution.py:277
  30.5 0.8 %shard_map.89 = (f32[1,32]{1,0:T(1,128)}, f32[1,64]{1,0:T(1,128)}) custom-call(f32[8,128]{1,0:T(8,128)S(1)} %bitcast.15, f32[8,64]{1,0:T(8,128)S(1)} %get-tuple-element.20.owner_ref, s32[1,64]{1,0:T(1,128)S(1)} %get-tuple-element.21.column_ref), custom_call_target="tpu_custom_call" | custom-call | tf_op jit(solution)/shard_map/pallas_call | solution.py:278
  (1 shorter events, 0.0 us)
Async XLA Ops:
  0.6 9.6 %collective-permute-start.1 = (bf16[1024,128]{1,0:T(8,128)(2,1)}, bf16[1024,128]{1,0:T(8,128)(2,1)S(1)}, u32[]{:S(2)}, u32[]{:S(2)}) collective-permute-start(bf16[1024,128]{1,0:T(8,128)(2,1)} %refs_2_.1), channel_id=1, source_target_pairs={{0,2},{1,3},{2,0},{3,1},{4,6},{5,7},{6,4},{7,5},{8,10},{9,11},{10,... | collective-permute-start | bytes 786440 | tf_op jit(solution)/shard_map/ppermute | solution.py:20
  3.7 11.4 %collective-permute-start = (bf16[1024,128]{1,0:T(8,128)(2,1)}, bf16[1024,128]{1,0:T(8,128)(2,1)S(1)}, u32[]{:S(2)}, u32[]{:S(2)}) collective-permute-start(bf16[1024,128]{1,0:T(8,128)(2,1)} %refs_2_.1), channel_id=1, source_target_pairs={{0,1},{1,0},{2,3},{3,2},{4,5},{5,4},{6,7},{7,6},{8,9},{9,8},{10,11... | collective-permute-start | bytes 786440 | tf_op jit(solution)/shard_map/ppermute | solution.py:20
  3.7 8.5 %collective-permute-start.2 = (bf16[1,32,128]{2,1,0:T(8,128)(2,1)}, bf16[1,32,128]{2,1,0:T(8,128)(2,1)S(1)}, u32[]{:S(2)}, u32[]{:S(2)}) collective-permute-start(bf16[1,32,128]{2,1,0:T(8,128)(2,1)} %bitcast.16), channel_id=1, source_target_pairs={{0,8},{4,12},{8,0},{12,4},{16,24},{20,28},{24,16},{28,20},{1,9},{5... | collective-permute-start | bytes 24584 | tf_op jit(solution)/shard_map/ppermute | solution.py:20
  5.2 6.9 %collective-permute-start.3 = (bf16[1,32,128]{2,1,0:T(8,128)(2,1)}, bf16[1,32,128]{2,1,0:T(8,128)(2,1)S(1)}, u32[]{:S(2)}, u32[]{:S(2)}) collective-permute-start(bf16[1,32,128]{2,1,0:T(8,128)(2,1)} %bitcast.17), channel_id=1, source_target_pairs={{0,16},{4,20},{8,24},{12,28},{16,0},{20,4},{24,8},{28,12},{1,17},{... | collective-permute-start | bytes 24584 | tf_op jit(solution)/shard_map/ppermute | solution.py:20
  7.8 5.7 %collective-permute-start.4 = (bf16[1,32,128]{2,1,0:T(8,128)(2,1)}, bf16[1,32,128]{2,1,0:T(8,128)(2,1)S(1)}, u32[]{:S(2)}, u32[]{:S(2)}) collective-permute-start(bf16[1,32,128]{2,1,0:T(8,128)(2,1)} %bitcast.18), channel_id=1, source_target_pairs={{0,24},{4,28},{8,16},{12,20},{16,8},{20,12},{24,0},{28,4},{1,25},{... | collective-permute-start | bytes 24584 | tf_op jit(solution)/shard_map/ppermute | solution.py:20
  10.2 7.3 %collective-permute-start.6 = (bf16[1024,128]{1,0:T(8,128)(2,1)S(1)}, bf16[1024,128]{1,0:T(8,128)(2,1)S(1)}, u32[]{:S(2)}, u32[]{:S(2)}) collective-permute-start(bf16[1024,128]{1,0:T(8,128)(2,1)S(1)} %collective-permute-done.1.refs_1_.refs_4_), channel_id=1, source_target_pairs={{0,1},{1,0},{2,3},{3,2},{4,5},{5,4},{6,7},{7,6},{8,9},{9,8},{10,11... | collective-permute-start | bytes 786440 | tf_op jit(solution)/shard_map/ppermute | solution.py:20
  10.2 3.3 %copy-start.1 = (bf16[1,1,32,128]{3,2,1,0:T(8,128)(2,1)S(1)}, bf16[1,1,32,128]{3,2,1,0:T(8,128)(2,1)}, u32[]{:S(2)}) copy-start(bf16[1,1,32,128]{3,2,1,0:T(8,128)(2,1)} %param.7) | copy-start | bytes 24580
  13.5 4.0 %collective-permute-start.5 = (bf16[4,32,128]{2,1,0:T(8,128)(2,1)S(1)}, bf16[4,32,128]{2,1,0:T(8,128)(2,1)S(1)}, u32[]{:S(2)}, u32[]{:S(2)}) collective-permute-start(bf16[4,32,128]{2,1,0:T(8,128)(2,1)S(1)} %pad_maximum_fusion), channel_id=1, source_target_pairs={{0,4},{4,0},{8,12},{12,8},{16,20},{20,16},{24,28},{28,24},{1,5},{5... | collective-permute-start | bytes 98312 | tf_op jit(solution)/shard_map/ppermute | solution.py:20
  15.1 2.4 %copy-start = (bf16[1024,128]{1,0:T(8,128)(2,1)S(1)}, bf16[1024,128]{1,0:T(8,128)(2,1)}, u32[]{:S(2)}) copy-start(bf16[1024,128]{1,0:T(8,128)(2,1)} %refs_2_.1) | copy-start | bytes 786436

commit v3 on v2

v3 whole, which is shorter than its diff:
```python
import functools

import jax
import jax.numpy as jnp
from jax import lax
from jax.experimental import pallas as pl
from jax.experimental.pallas import tpu as pltpu
from jax.sharding import PartitionSpec as P


FAR_BELOW = -1e30
LANES = 128
LOW = 256
BOOK_CHUNK = 256
PASSAGES = 4
EMBED = (2, 4, 2)
STEPS = lambda high: [high[i : i + 2] for i in range(0, len(high), 2)]


def exchange(value, axis, mask):
    count = lax.axis_size(axis)
    return lax.ppermute(value, axis, [(i, i ^ mask) for i in range(count)])


def steps_of(count):
    high = [1 << i for i in range(1, count.bit_length() - 1)]
    return STEPS(high) + [[1]] if count > 1 else []


def gather_by_xor(block, axis):
    parts = [block[None]]
    for bits in steps_of(lax.axis_size(axis)):
        held = jnp.concatenate(parts, axis=0)
        parts = [held]
        masks = [0]
        for bit in bits:
            masks += [mask | bit for mask in masks]
        sent = {}
        for mask in masks[:0:-1]:
            sent[mask] = exchange(held, axis, mask)
        parts += [sent[mask] for mask in masks[1:]]
    return parts


def owner_mask(place, count):
    bits = sum(steps_of(count), [])
    return sum((((place >> i) & 1) * bit for i, bit in enumerate(bits)), place * 0)


def named_rows(total, onehot, high, book_ref, first):
    for j in range(0, book_ref.shape[0] // LOW, 2):
        pair = jnp.concatenate(
            [book_ref[(j + h) * LOW : (j + h + 1) * LOW, :] for h in range(2)], axis=1
        )
        found = jnp.dot(onehot, pair, preferred_element_type=jnp.float32)
        for h in range(2):
            total = jnp.where(high == first + (j + h), found[:, h * LANES : (h + 1) * LANES], total)
    return total


def first_of(k, book_ref):
    return (lax.axis_index("rep") ^ k) * (book_ref.shape[0] // LOW)


def embed(total_ref, sum_ref, onehot_ref, high_ref, blocks, passages, slots, together):
    many = max(n for n in range(1, together + 1) if passages % n == 0) * slots
    for start in range(0, passages * slots, many):
        here = pl.ds(start, many)
        total = jnp.zeros((many, LANES), jnp.float32) if sum_ref is None else sum_ref[here, :]
        for k, book_ref in blocks:
            total = named_rows(total, onehot_ref[here, :], high_ref[here, :], book_ref, first_of(k, book_ref))
        total_ref[here, :] = total.astype(total_ref.dtype)


def prepare_kernel(
    tokens, near, ids_hbm, own_hbm, weight_hbm, length_hbm, cands_hbm, *refs
):
    near_refs = refs[: len(near)]
    onehot_ref, high_ref, sum_ref, live_ref, mine_ref, owner_ref, column_ref = refs[len(near) : len(near) + 7]
    own_ref, weight_ref, ids_ref, length_ref, cands_ref, sems = refs[len(near) + 7 :]
    copies = [
        pltpu.make_async_copy(source, place, sems.at[i])
        for i, (source, place) in enumerate(
            (
                (ids_hbm, ids_ref),
                (length_hbm, length_ref),
                (cands_hbm, cands_ref),
                (weight_hbm, weight_ref),
                (own_hbm, own_ref),
            )
        )
    ]
    for copy in copies:
        copy.start()
    passages, slots = ids_ref.shape
    shape = mine_ref.shape
    shard = lax.axis_index("shard")
    mask = owner_mask(lax.broadcasted_iota(jnp.int32, shape, 1) // tokens, shape[0])
    mine_ref[...] = ((lax.broadcasted_iota(jnp.int32, shape, 0) ^ shard) == mask).astype(jnp.float32)
    copies[0].wait()
    ids_by_slot = jnp.transpose(ids_ref[...])
    lane = lax.broadcasted_iota(jnp.int32, (slots, LANES), 1)
    for p in range(passages):
        here = pl.ds(p * slots, slots)
        ids = jnp.broadcast_to(ids_by_slot[:, p : p + 1], (slots, LANES))
        low = ids & (LOW - 1)
        onehot_ref[here, :] = jnp.concatenate(
            [(low == lane + k * LANES).astype(jnp.float32) for k in range(LOW // LANES)], axis=1
        ).astype(jnp.bfloat16)
        high_ref[here, :] = ids >> (LOW.bit_length() - 1)
    embed(sum_ref, None, onehot_ref, high_ref, list(zip(near, near_refs)), passages, slots, EMBED[0])
    for copy in copies[1:]:
        copy.wait()
    for p in range(passages):
        live_ref[p : p + 1, :] = jnp.broadcast_to(length_ref[:, p : p + 1], (1, live_ref.shape[1]))
    cands = cands_ref[...]
    wanted = cands.shape[1]
    owner_ref[...] = jnp.zeros(owner_ref.shape, jnp.float32)
    owner_ref[:, 0:wanted] = (
        lax.broadcasted_iota(jnp.int32, (shape[0], wanted), 0) == cands // passages
    ).astype(jnp.float32)
    column_ref[...] = jnp.zeros(column_ref.shape, jnp.int32)
    column_ref[:, 0:wanted] = jnp.broadcast_to(tokens + cands % passages, (shape[0], wanted))


def fold_kernel(blocks, weight_ref, codes_hbm, onehot_ref, high_ref, sum_ref, *refs):
    *book_refs, out_ref, residual_ref, codes_ref, sem = refs
    copy = pltpu.make_async_copy(codes_hbm, codes_ref, sem)
    copy.start()
    passages, slots, _ = codes_ref.shape
    embed(out_ref, sum_ref, onehot_ref, high_ref, list(zip(blocks, book_refs)), passages, slots, EMBED[1])
    levels = weight_ref.shape[1]
    values = [jnp.broadcast_to(weight_ref[:, k : k + 1], (slots, LANES)) for k in range(levels)]
    copy.wait()
    for p in range(passages):
        codes = codes_ref[p]
        residual = values[levels - 1]
        for level in range(levels - 2, -1, -1):
            residual = jnp.where(codes == level, values[level], residual)
        residual_ref[pl.ds(p * slots, slots), :] = residual


def exact_dot(selector, values):
    selector = selector.astype(jnp.bfloat16)
    total = None
    for _ in range(3):
        term = values.astype(jnp.bfloat16)
        values = values - term.astype(jnp.float32)
        found = lax.dot_general(
            selector, term, (((1,), (1,)), ((), ())), preferred_element_type=jnp.float32
        )
        total = found if total is None else total + found
    return total


def scored(tokens, queries, mine, live_ref, embedded_ref, book_refs, room):
    width = queries.shape[0]
    passages = live_ref.shape[0]
    slots = embedded_ref.shape[0] // passages

    nothing = jnp.zeros_like(queries)
    diagonal = jnp.concatenate(
        [jnp.concatenate([queries, nothing], axis=1), jnp.concatenate([nothing, queries], axis=1)], axis=0
    )

    def products(one, two):
        return lax.dot_general(
            jnp.concatenate([one, two], axis=1),
            diagonal,
            (((1,), (1,)), ((), ())),
            preferred_element_type=jnp.float32,
        )

    best = jnp.full((8, 2 * width), FAR_BELOW, jnp.float32)
    for book_ref in book_refs:
        half = book_ref.shape[0] // 2
        chunk = min(BOOK_CHUNK, half)
        for c in range(0, half, chunk):
            found = products(book_ref[c : c + chunk, :], book_ref[half + c : half + c + chunk, :])
            best = jnp.maximum(best, jnp.max(found.reshape(chunk // 8, 8, 2 * width), axis=0))
    best = jnp.max(best, axis=0, keepdims=True)
    best = jnp.maximum(best[:, :width], best[:, width:])
    slot = lax.broadcasted_iota(jnp.int32, (slots, 2 * width), 0)
    half = passages // 2
    tops = [None] * passages
    many = max(n for n in range(1, PASSAGES + 1) if half % n == 0)
    for start in range(0, half, many):
        one, two = (embedded_ref[q * slots : (q + many) * slots, :] for q in (start, start + half))
        together = products(one, two)
        for p in range(start, start + many):
            live = jnp.concatenate([live_ref[q : q + 1, 0:width] for q in (p, p + half)], axis=1)
            found = together[(p - start) * slots : (p - start + 1) * slots, :]
            found = jnp.max(jnp.where(slot < live, found, FAR_BELOW), axis=0, keepdims=True)
            tops[p], tops[p + half] = found[:, :width], found[:, width:]
    table = jnp.concatenate(
        [jnp.zeros((tokens, width), jnp.float32)]
        + tops
        + [jnp.zeros((room - tokens - passages, width), jnp.float32)],
        axis=0,
    )
    sums = exact_dot(mine, table)
    kept = mine * best
    while kept.shape[1] > LANES:
        half = kept.shape[1] // 2
        kept = kept[:, :half] + kept[:, half:]
    shift = kept.shape[1] // 2
    while shift >= tokens:
        kept = kept + pltpu.roll(kept, shift, 1)
        shift //= 2
    where = lax.broadcasted_iota(jnp.int32, kept.shape, 1)
    return jnp.where(where < tokens, kept, sums)


def early_kernel(
    tokens, last, live_ref, mine_ref, onehot_ref, high_ref, residual_ref, sum_ref, query_ref, *refs
):
    *book_refs, out_ref, embedded_ref = refs
    passages = live_ref.shape[0]
    slots = sum_ref.shape[0] // passages

    @pl.when(pl.program_id(0) == 0)
    def _():
        many = max(n for n in range(1, EMBED[2] + 1) if passages % n == 0) * slots
        for start in range(0, passages * slots, many):
            here = pl.ds(start, many)
            total = sum_ref[here, :]
            for k in last:
                book_ref = book_refs[k]
                total = named_rows(total, onehot_ref[here, :], high_ref[here, :], book_ref, first_of(k, book_ref))
            embedded_ref[here, :] = (total + residual_ref[here, :]).astype(jnp.bfloat16)
        out_ref[...] = jnp.zeros(out_ref.shape, jnp.float32)

    room = out_ref.shape[1]
    out_ref[...] += scored(tokens, query_ref[...], mine_ref[...], live_ref, embedded_ref, book_refs, room)


def late_kernel(tokens, live_ref, mine_ref, embedded_ref, early_ref, query_ref, *refs):
    *book_refs, out_ref = refs

    @pl.when(pl.program_id(0) == 0)
    def _():
        out_ref[...] = early_ref[...]

    room = out_ref.shape[1]
    out_ref[...] += scored(tokens, query_ref[...], mine_ref[...], live_ref, embedded_ref, book_refs, room)


def finish_kernel(tokens, table_ref, owner_ref, column_ref, best_ref, scores_ref):
    table = table_ref[...]
    best_ref[...] = jnp.max(table, axis=0, keepdims=True)[:, 0:tokens]
    found = jnp.take_along_axis(table, column_ref[...], axis=1)
    found = jnp.sum(found * owner_ref[...], axis=0, keepdims=True)
    scores_ref[...] = found[:, 0 : scores_ref.shape[1]]


def on_device(queries, candidates, codebook, bucket_weights, centroid_ids, residual_codes, passage_lengths):
    tokens, features = queries.shape[2:]
    passages, slots = centroid_ids.shape
    wanted = candidates.shape[2]
    shards, reps = lax.axis_size("shard"), lax.axis_size("rep")
    vmem = pl.BlockSpec(memory_space=pltpu.VMEM)
    rows = passages * slots
    width = min(LANES, max(shards // 2, 1) * tokens)
    room = LANES

    books = {0: codebook}
    bit = reps // 2
    while bit:
        for k in list(books):
            books[k ^ bit] = exchange(books[k], "rep", bit)
        bit //= 2
    near = tuple(k for k in (1,) if k < reps)
    last = tuple(k for k in (reps - 1,) if k > 1)
    middle = tuple(k for k in range(reps) if k not in near + last)

    def shaped(*shape, dtype=jnp.float32):
        return jax.ShapeDtypeStruct(shape, dtype)

    def kernel(body, limit=24, **more):
        return pl.pallas_call(
            body,
            compiler_params=pltpu.CompilerParams(vmem_limit_bytes=limit << 20),
            cost_estimate=pl.CostEstimate(flops=1 << 30, bytes_accessed=2 << 20, transcendentals=0),
            **more,
        )

    hbm = pl.BlockSpec(memory_space=pltpu.HBM)

    def in_hbm(value):
        return pltpu.with_memory_space_constraint(value, pltpu.HBM)

    onehot, high, total, live, mine, owner, column, own, weights = kernel(
        functools.partial(prepare_kernel, tokens, near),
        out_shape=(
            shaped(rows, LOW, dtype=jnp.bfloat16),
            shaped(rows, LANES, dtype=jnp.int32),
            shaped(rows, features),
            shaped(passages, width, dtype=jnp.int32),
            shaped(shards, shards * tokens),
            shaped(shards, room),
            shaped(shards, room, dtype=jnp.int32),
            shaped(*codebook.shape, dtype=codebook.dtype),
            shaped(1, bucket_weights.shape[0]),
        ),
        in_specs=[hbm] * 5 + [vmem] * len(near),
        out_specs=(vmem,) * 9,
        scratch_shapes=[
            pltpu.VMEM(centroid_ids.shape, jnp.int32),
            pltpu.VMEM((1, passages), jnp.int32),
            pltpu.VMEM((1, wanted), jnp.int32),
            pltpu.SemaphoreType.DMA((5,)),
        ],
    )(
        *map(
            in_hbm,
            (
                centroid_ids,
                codebook,
                bucket_weights.reshape(1, -1),
                passage_lengths.reshape(1, passages),
                candidates[0],
            ),
        ),
        *[books[k] for k in near],
    )
    books[0] = own
    first, *others = [part.reshape(-1, features) for part in gather_by_xor(queries[0, 0], "shard")]
    total, residual = kernel(
        functools.partial(fold_kernel, middle),
        out_shape=(shaped(rows, features), shaped(rows, features)),
        in_specs=[vmem, hbm] + [vmem] * (3 + len(middle)),
        out_specs=(vmem, vmem),
        scratch_shapes=[pltpu.VMEM(residual_codes.shape, jnp.int32), pltpu.SemaphoreType.DMA],
    )(
        weights,
        in_hbm(residual_codes),
        onehot,
        high,
        total,
        *[books[k] for k in middle],
    )

    def queries_spec(start):
        steps = start // width
        return [
            pl.BlockSpec((shards, width), lambda i: (0, i + steps)),
            pl.BlockSpec((width, features), lambda i: (i, 0)),
        ]

    mine_spec, query_spec = queries_spec(0)
    blocks = [books[k] for k in range(reps)]
    packed, embedded = kernel(
        functools.partial(early_kernel, tokens, last),
        out_shape=(shaped(shards, room), shaped(rows, features, dtype=jnp.bfloat16)),
        grid=(first.shape[0] // width,),
        in_specs=[vmem, mine_spec] + [vmem] * 4 + [query_spec] + [vmem] * reps,
        out_specs=(vmem, vmem),
    )(live, mine, onehot, high, residual, total, first, *blocks)
    for other in others:
        mine_spec, query_spec = queries_spec(first.shape[0])
        packed = kernel(
            functools.partial(late_kernel, tokens),
            out_shape=shaped(shards, room),
            grid=(other.shape[0] // width,),
            in_specs=[vmem, mine_spec, vmem, vmem, query_spec] + [vmem] * reps,
            out_specs=vmem,
        )(live, mine, embedded, packed, other, *blocks)

    table = lax.all_to_all(packed, "shard", split_axis=0, concat_axis=0, tiled=True)
    best, scores = pl.pallas_call(
        functools.partial(finish_kernel, tokens),
        out_shape=(shaped(1, tokens), shaped(1, wanted)),
        in_specs=[vmem] * 3,
        out_specs=(vmem, vmem),
        compiler_params=pltpu.CompilerParams(vmem_limit_bytes=4 << 20),
    )(table, owner, column)
    return best[None], scores[None]


def solution(mesh):
    in_specs = (
        P("rep", "shard", None, None),
        P("rep", "shard", None),
        P(("shard", "rep"), None),
        P(),
        P("shard", None),
        P("shard", None, None),
        P("shard"),
    )
    out_specs = (P("rep", "shard", None), P("rep", "shard", None))

    return jax.shard_map(on_device, mesh=mesh, in_specs=in_specs, out_specs=out_specs, check_vma=False)
```

time: 31.5 us -> 30.9 us (0.981)
  blocking collectives: 11.1 us -> 8.88 us
  waiting for transfers between devices: 4.08 us -> 5.44 us
  other arithmetic: 0.01 us -> 0.7 us
  Pallas kernels: 6.43 us -> 5.95 us
    all_to_all x1, blocking collectives: 11.1 us -> 8.88 us  [on_device(): lax.all_to_all(packed, 'shard', split_axis=0, concat_axis=0, tiled=True)]
    ppermute x7, waiting for transfers between devices: 4.08 us -> 5.44 us  [exchange(): return lax.ppermute(value, axis, [(i, i ^ mask) for i in range(count)])]
    concatenate x1, other arithmetic: 0.01 us -> 0.7 us  [gather_by_xor(): held = jnp.concatenate(parts, axis=0)]
    pallas_call x2 -> x3, Pallas kernels: 3.89 us -> 3.86 us  [the longest x1 1.73 us: on_device(): kernel(functools.partial(prepare_kernel, tokens, near), out_shape=(shaped...]
  transfers between devices with their start and end apart: 7 -> 7, of which waited for: 3 -> 2; matrix products, arithmetic and copies ran while one was open for 0% -> 2% of each run, Pallas kernels for 12% -> 15%
where the time goes in v3:
time: 30.9 us; the launch traced here: 30.6 us
  starting transfers between devices  8.94 us (29%)
  blocking collectives  8.88 us (29%)
  Pallas kernels  5.95 us (19%)
  waiting for transfers between devices  5.44 us (18%)
  other arithmetic  0.7 us (2%)
  between operations  0.67 us (2%)
    ppermute x7, starting transfers between devices, exchange(): return lax.ppermute(value, axis, [(i, i ^ mask) for i in range(count)])  8.94 us
    all_to_all x1, blocking collectives, on_device(): lax.all_to_all(packed, 'shard', split_axis=0, concat_axis=0, tiled=True)  8.88 us
    ppermute x7, waiting for transfers between devices, exchange(): return lax.ppermute(value, axis, [(i, i ^ mask) for i in range(count)])  5.44 us
    pallas_call x1, Pallas kernels, on_device(): kernel(functools.partial(prepare_kernel, tokens, near), out_shape=(shaped...  1.73 us
    pallas_call x1, Pallas kernels, on_device(): kernel(functools.partial(fold_kernel, middle), out_shape=(shaped(rows, fe...  1.5 us
    pallas_call x1, Pallas kernels, on_device(): kernel(functools.partial(early_kernel, tokens, last), out_shape=(shaped(s...  1.35 us
    pallas_call x1, Pallas kernels, on_device(): kernel(functools.partial(late_kernel, tokens), out_shape=shaped(shards, r...  0.78 us
    concatenate x1, other arithmetic, gather_by_xor(): held = jnp.concatenate(parts, axis=0)  0.7 us
  transfers between devices with their start and end apart: 7, of which 2 were waited for; matrix products, arithmetic and copies ran while one was open for 2% of the time, Pallas kernels for 15%

profile of v3, /device:TPU:0, one launch (start us, length us, event | category | flops | bytes accessed | tf_op | source)
XLA Modules:
  0.0 30.6 jit_solution(7377174341540395100)
XLA Ops:
  0.6 3.0 %collective-permute-start.1 = (bf16[1024,128]{1,0:T(8,128)(2,1)}, bf16[1024,128]{1,0:T(8,128)(2,1)S(1)}, u32[]{:S(2)}, u32[]{:S(2)}) collective-permute-start(bf16[1024,128]{1,0:T(8,128)(2,1)} %own_hbm.1), channel_id=1, source_target_pairs={{0,2},{1,3},{2,0},{3,1},{4,6},{5,7},{6,4},{7,5},{8,10},{9,11},{10,... | collective-permute-start | bytes 786440 | tf_op jit(solution)/shard_map/ppermute | solution.py:22
  3.7 0.0 collective-permute-start
  3.7 1.6 %collective-permute-start.2 = (bf16[1,32,128]{2,1,0:T(8,128)(2,1)}, bf16[1,32,128]{2,1,0:T(8,128)(2,1)S(1)}, u32[]{:S(2)}, u32[]{:S(2)}) collective-permute-start(bf16[1,32,128]{2,1,0:T(8,128)(2,1)} %bitcast.16), channel_id=1, source_target_pairs={{0,8},{4,12},{8,0},{12,4},{16,24},{20,28},{24,16},{28,20},{1,9},{5... | collective-permute-start | bytes 24584 | tf_op jit(solution)/shard_map/ppermute | solution.py:22
  5.2 2.6 %collective-permute-start.3 = (bf16[1,32,128]{2,1,0:T(8,128)(2,1)}, bf16[1,32,128]{2,1,0:T(8,128)(2,1)S(1)}, u32[]{:S(2)}, u32[]{:S(2)}) collective-permute-start(bf16[1,32,128]{2,1,0:T(8,128)(2,1)} %bitcast.17), channel_id=1, source_target_pairs={{0,16},{4,20},{8,24},{12,28},{16,0},{20,4},{24,8},{28,12},{1,17},{... | collective-permute-start | bytes 24584 | tf_op jit(solution)/shard_map/ppermute | solution.py:22
  7.8 0.2 collective-permute-start.4
  8.1 2.1 %collective-permute-done.1.refs_1_.refs_2_ = bf16[1024,128]{1,0:T(8,128)(2,1)S(1)} collective-permute-done((bf16[1024,128]{1,0:T(8,128)(2,1)}, bf16[1024,128]{1,0:T(8,128)(2,1)S(1)}, u32[]{:S(2)}, u32[]{:S(2)}) %collective-permute-start.1) | collective-permute-done | bytes 262176 | tf_op jit(solution)/shard_map/ppermute | solution.py:22
  10.2 0.0 collective-permute-start.5
  10.2 0.0 collective-permute-done.2
  10.2 0.0 collective-permute-done.3
  10.2 3.3 %collective-permute-done.4 = bf16[1,32,128]{2,1,0:T(8,128)(2,1)S(1)} collective-permute-done((bf16[1,32,128]{2,1,0:T(8,128)(2,1)}, bf16[1,32,128]{2,1,0:T(8,128)(2,1)S(1)}, u32[]{:S(2)}, u32[]{:S(2)}) %collective-permute-start.4) | collective-permute-done | bytes 8224 | tf_op jit(solution)/shard_map/ppermute | solution.py:22
  13.5 0.7 %pad_maximum_fusion = bf16[4,32,128]{2,1,0:T(8,128)(2,1)S(1)} fusion(bf16[1,32,128]{2,1,0:T(8,128)(2,1)S(1)} %collective-permute-done.4, bf16[1,32,128]{2,1,0:T(8,128)(2,1)S(1)} %collective-permute-done.3, bf16[1,32,128]{2,1,0:T(8,128)(2,1)S(1)} %collective-permute-done.2, bf16[1,32,128]{2,1,0:T(8,128)(2,1)} %bitcast.19), kind=kLoop, calls=%fused_computation | loop fusion | flops 49152 | bytes 65536 | tf_op jit(solution)/shard_map/concatenate | solution.py:33
  14.2 1.5 %collective-permute-start.6 = (bf16[4,32,128]{2,1,0:T(8,128)(2,1)S(1)}, bf16[4,32,128]{2,1,0:T(8,128)(2,1)S(1)}, u32[]{:S(2)}, u32[]{:S(2)}) collective-permute-start(bf16[4,32,128]{2,1,0:T(8,128)(2,1)S(1)} %pad_maximum_fusion), channel_id=1, source_target_pairs={{0,4},{4,0},{8,12},{12,8},{16,20},{20,16},{24,28},{28,24},{1,5},{5... | collective-permute-start | bytes 98312 | tf_op jit(solution)/shard_map/ppermute | solution.py:22
  15.7 0.0 collective-permute-done.refs_0_.refs_1_
  15.7 1.7 %shard_map.86 = (bf16[2048,256]{1,0:T(8,128)(2,1)S(1)}, s32[2048,128]{1,0:T(8,128)S(1)}, f32[2048,128]{1,0:T(8,128)S(1)}, s32[16,128]{1,0:T(8,128)S(1)}, f32[8,2...) custom-call(s32[16,128]{1,0:T(8,128)} %ids_hbm.1, ...), custom_call_target="tpu_custom_call" | custom-call | flops 1073741824 | bytes 2097152 | tf_op jit(solution)/shard_map/pallas_call | solution.py:292
  17.5 1.5 %shard_map.87 = (f32[2048,128]{1,0:T(8,128)S(1)}, f32[2048,128]{1,0:T(8,128)S(1)}) custom-call(f32[1,4]{1,0:T(1,128)S(1)} %get-tuple-element.21.weight_ref, s32[16,128,128]{2,1,0:T(8,128)} %codes_hbm.1, bf16[2048,256]{1,0:T(8,128)(2,1)S(1)} %get-tuple-element.19.onehot_ref, s32[2048,128]{1,0:T(8,128)S(1)} %get-tuple-element.20.high_ref, ...), custom_call_target="tpu_custom_call" | custom-call | flops 1073741824 | bytes 2097152 | tf_op jit(solution)/shard_map/pallas_call | solution.py:328
  19.0 0.0 collective-permute-done.5.refs_3_
  19.0 1.3 %shard_map.88 = (f32[8,128]{1,0:T(8,128)S(1)}, bf16[2048,128]{1,0:T(8,128)(2,1)S(1)}) custom-call(s32[16,128]{1,0:T(8,128)S(1)} %get-tuple-element.17.live_ref, f32[8,256]{1,0:T(8,128)S(1)} %get-tuple-element.18.mine_ref, bf16[2048,256]{1,0:T(8,128)(2,1)S(1)} %get-tuple-element.19.onehot_ref, s32[2048,128]{1,0:T(8,128)S(1)} %get-tuple-element.20.high_ref, ...), custom_call_target="tpu_custom_call" | custom-call | flops 1073741824 | bytes 2097152 | tf_op jit(solution)/shard_map/pallas_call | solution.py:352
  20.3 0.0 collective-permute-done.6
  20.3 0.8 %shard_map.89 = f32[8,128]{1,0:T(8,128)S(1)} custom-call(s32[16,128]{1,0:T(8,128)S(1)} %get-tuple-element.17.live_ref, f32[8,256]{1,0:T(8,128)S(1)} %get-tuple-element.18.mine_ref, bf16[2048,128]{1,0:T(8,128)(2,1)S(1)} %get-tuple-element.26.embedded_ref, f32[8,128]{1,0:T(8,128)S(1)} %get-tuple-element.27.early_ref, bf16[128,128]{1,0:T(8,128)(2,1)S(1)} %bitcast.15, ...), custom_call_target="tpu_custom_call" | custom-call | flops 1073741824 | bytes 2097152 | tf_op jit(solution)/shard_map/pallas_call | solution.py:361
  21.1 8.9 %all_to_all.11 = f32[8,1,128]{2,1,0:T(1,128)S(1)} all-to-all(f32[8,1,128]{2,1,0:T(1,128)S(1)} %bitcast.14), channel_id=1, replica_groups=mesh['shard'=8,'rep'=4] {'shard'}, dimensions={0} | all-to-all | bytes 8192 | tf_op jit(solution)/shard_map/all_to_all | solution.py:369
  30.0 0.6 %shard_map.90 = (f32[1,32]{1,0:T(1,128)}, f32[1,64]{1,0:T(1,128)}) custom-call(f32[8,128]{1,0:T(8,128)S(1)} %bitcast.13, f32[8,128]{1,0:T(8,128)S(1)} %get-tuple-element.28.owner_ref, s32[8,128]{1,0:T(8,128)S(1)} %get-tuple-element.29.column_ref), custom_call_target="tpu_custom_call" | custom-call | tf_op jit(solution)/shard_map/pallas_call | solution.py:370
Async XLA Ops:
  0.6 9.6 %collective-permute-start.1 = (bf16[1024,128]{1,0:T(8,128)(2,1)}, bf16[1024,128]{1,0:T(8,128)(2,1)S(1)}, u32[]{:S(2)}, u32[]{:S(2)}) collective-permute-start(bf16[1024,128]{1,0:T(8,128)(2,1)} %own_hbm.1), channel_id=1, source_target_pairs={{0,2},{1,3},{2,0},{3,1},{4,6},{5,7},{6,4},{7,5},{8,10},{9,11},{10,... | collective-permute-start | bytes 786440 | tf_op jit(solution)/shard_map/ppermute | solution.py:22
  3.7 12.1 %collective-permute-start = (bf16[1024,128]{1,0:T(8,128)(2,1)}, bf16[1024,128]{1,0:T(8,128)(2,1)S(1)}, u32[]{:S(2)}, u32[]{:S(2)}) collective-permute-start(bf16[1024,128]{1,0:T(8,128)(2,1)} %own_hbm.1), channel_id=1, source_target_pairs={{0,1},{1,0},{2,3},{3,2},{4,5},{5,4},{6,7},{7,6},{8,9},{9,8},{10,11... | collective-permute-start | bytes 786440 | tf_op jit(solution)/shard_map/ppermute | solution.py:22
  3.7 6.5 %collective-permute-start.2 = (bf16[1,32,128]{2,1,0:T(8,128)(2,1)}, bf16[1,32,128]{2,1,0:T(8,128)(2,1)S(1)}, u32[]{:S(2)}, u32[]{:S(2)}) collective-permute-start(bf16[1,32,128]{2,1,0:T(8,128)(2,1)} %bitcast.16), channel_id=1, source_target_pairs={{0,8},{4,12},{8,0},{12,4},{16,24},{20,28},{24,16},{28,20},{1,9},{5... | collective-permute-start | bytes 24584 | tf_op jit(solution)/shard_map/ppermute | solution.py:22
  5.2 4.9 %collective-permute-start.3 = (bf16[1,32,128]{2,1,0:T(8,128)(2,1)}, bf16[1,32,128]{2,1,0:T(8,128)(2,1)S(1)}, u32[]{:S(2)}, u32[]{:S(2)}) collective-permute-start(bf16[1,32,128]{2,1,0:T(8,128)(2,1)} %bitcast.17), channel_id=1, source_target_pairs={{0,16},{4,20},{8,24},{12,28},{16,0},{20,4},{24,8},{28,12},{1,17},{... | collective-permute-start | bytes 24584 | tf_op jit(solution)/shard_map/ppermute | solution.py:22
  7.8 5.7 %collective-permute-start.4 = (bf16[1,32,128]{2,1,0:T(8,128)(2,1)}, bf16[1,32,128]{2,1,0:T(8,128)(2,1)S(1)}, u32[]{:S(2)}, u32[]{:S(2)}) collective-permute-start(bf16[1,32,128]{2,1,0:T(8,128)(2,1)} %bitcast.18), channel_id=1, source_target_pairs={{0,24},{4,28},{8,16},{12,20},{16,8},{20,12},{24,0},{28,4},{1,25},{... | collective-permute-start | bytes 24584 | tf_op jit(solution)/shard_map/ppermute | solution.py:22
  10.2 8.8 %collective-permute-start.5 = (bf16[1024,128]{1,0:T(8,128)(2,1)S(1)}, bf16[1024,128]{1,0:T(8,128)(2,1)S(1)}, u32[]{:S(2)}, u32[]{:S(2)}) collective-permute-start(bf16[1024,128]{1,0:T(8,128)(2,1)S(1)} %collective-permute-done.1.refs_1_.refs_2_), channel_id=1, source_target_pairs={{0,1},{1,0},{2,3},{3,2},{4,5},{5,4},{6,7},{7,6},{8,9},{9,8},{10,11... | collective-permute-start | bytes 786440 | tf_op jit(solution)/shard_map/ppermute | solution.py:22
  14.2 6.1 %collective-permute-start.6 = (bf16[4,32,128]{2,1,0:T(8,128)(2,1)S(1)}, bf16[4,32,128]{2,1,0:T(8,128)(2,1)S(1)}, u32[]{:S(2)}, u32[]{:S(2)}) collective-permute-start(bf16[4,32,128]{2,1,0:T(8,128)(2,1)S(1)} %pad_maximum_fusion), channel_id=1, source_target_pairs={{0,4},{4,0},{8,12},{12,8},{16,20},{20,16},{24,28},{28,24},{1,5},{5... | collective-permute-start | bytes 98312 | tf_op jit(solution)/shard_map/ppermute | solution.py:22

commit v4 on v3

--- a/solution.py
+++ b/solution.py
@@ -141,16 +141,16 @@
 
 
 def exact_dot(selector, values):
-    selector = selector.astype(jnp.bfloat16)
-    total = None
+    terms = []
     for _ in range(3):
-        term = values.astype(jnp.bfloat16)
-        values = values - term.astype(jnp.float32)
-        found = lax.dot_general(
-            selector, term, (((1,), (1,)), ((), ())), preferred_element_type=jnp.float32
-        )
-        total = found if total is None else total + found
-    return total
+        terms.append(values.astype(jnp.bfloat16))
+        values = values - terms[-1].astype(jnp.float32)
+    return lax.dot_general(
+        jnp.concatenate([selector.astype(jnp.bfloat16)] * 3, axis=1),
+        jnp.concatenate(terms, axis=1),
+        (((1,), (1,)), ((), ())),
+        preferred_element_type=jnp.float32,
+    )
 
 
 def scored(tokens, queries, mine, live_ref, embedded_ref, book_refs, room):

time: 30.9 us -> 30.8 us (level)
  no operation moved by 1% of the time
where the time goes in v4:
time: 30.8 us; the launch traced here: 30.5 us
  starting transfers between devices  8.94 us (29%)
  blocking collectives  8.87 us (29%)
  Pallas kernels  5.93 us (19%)
  waiting for transfers between devices  5.44 us (18%)
  other arithmetic  0.7 us (2%)
  between operations  0.67 us (2%)
    ppermute x7, starting transfers between devices, exchange(): return lax.ppermute(value, axis, [(i, i ^ mask) for i in range(count)])  8.94 us
    all_to_all x1, blocking collectives, on_device(): lax.all_to_all(packed, 'shard', split_axis=0, concat_axis=0, tiled=True)  8.87 us
    ppermute x7, waiting for transfers between devices, exchange(): return lax.ppermute(value, axis, [(i, i ^ mask) for i in range(count)])  5.44 us
    pallas_call x1, Pallas kernels, on_device(): kernel(functools.partial(prepare_kernel, tokens, near), out_shape=(shaped...  1.73 us
    pallas_call x1, Pallas kernels, on_device(): kernel(functools.partial(fold_kernel, middle), out_shape=(shaped(rows, fe...  1.5 us
    pallas_call x1, Pallas kernels, on_device(): kernel(functools.partial(early_kernel, tokens, last), out_shape=(shaped(s...  1.35 us
    pallas_call x1, Pallas kernels, on_device(): kernel(functools.partial(late_kernel, tokens), out_shape=shaped(shards, r...  0.77 us
    concatenate x1, other arithmetic, gather_by_xor(): held = jnp.concatenate(parts, axis=0)  0.7 us
  transfers between devices with their start and end apart: 7, of which 2 were waited for; matrix products, arithmetic and copies ran while one was open for 2% of the time, Pallas kernels for 15%

profile of v4, /device:TPU:0, one launch (start us, length us, event | category | flops | bytes accessed | tf_op | source)
XLA Modules:
  0.0 30.5 jit_solution(13207145537467655473)
XLA Ops:
  0.6 3.0 %collective-permute-start.1 = (bf16[1024,128]{1,0:T(8,128)(2,1)}, bf16[1024,128]{1,0:T(8,128)(2,1)S(1)}, u32[]{:S(2)}, u32[]{:S(2)}) collective-permute-start(bf16[1024,128]{1,0:T(8,128)(2,1)} %own_hbm.1), channel_id=1, source_target_pairs={{0,2},{1,3},{2,0},{3,1},{4,6},{5,7},{6,4},{7,5},{8,10},{9,11},{10,... | collective-permute-start | bytes 786440 | tf_op jit(solution)/shard_map/ppermute | solution.py:22
  3.7 0.0 collective-permute-start
  3.7 1.6 %collective-permute-start.2 = (bf16[1,32,128]{2,1,0:T(8,128)(2,1)}, bf16[1,32,128]{2,1,0:T(8,128)(2,1)S(1)}, u32[]{:S(2)}, u32[]{:S(2)}) collective-permute-start(bf16[1,32,128]{2,1,0:T(8,128)(2,1)} %bitcast.16), channel_id=1, source_target_pairs={{0,8},{4,12},{8,0},{12,4},{16,24},{20,28},{24,16},{28,20},{1,9},{5... | collective-permute-start | bytes 24584 | tf_op jit(solution)/shard_map/ppermute | solution.py:22
  5.2 2.6 %collective-permute-start.3 = (bf16[1,32,128]{2,1,0:T(8,128)(2,1)}, bf16[1,32,128]{2,1,0:T(8,128)(2,1)S(1)}, u32[]{:S(2)}, u32[]{:S(2)}) collective-permute-start(bf16[1,32,128]{2,1,0:T(8,128)(2,1)} %bitcast.17), channel_id=1, source_target_pairs={{0,16},{4,20},{8,24},{12,28},{16,0},{20,4},{24,8},{28,12},{1,17},{... | collective-permute-start | bytes 24584 | tf_op jit(solution)/shard_map/ppermute | solution.py:22
  7.8 0.2 collective-permute-start.4
  8.1 2.1 %collective-permute-done.1.refs_1_.refs_2_ = bf16[1024,128]{1,0:T(8,128)(2,1)S(1)} collective-permute-done((bf16[1024,128]{1,0:T(8,128)(2,1)}, bf16[1024,128]{1,0:T(8,128)(2,1)S(1)}, u32[]{:S(2)}, u32[]{:S(2)}) %collective-permute-start.1) | collective-permute-done | bytes 262176 | tf_op jit(solution)/shard_map/ppermute | solution.py:22
  10.2 0.0 collective-permute-start.5
  10.2 0.0 collective-permute-done.2
  10.2 0.0 collective-permute-done.3
  10.2 3.3 %collective-permute-done.4 = bf16[1,32,128]{2,1,0:T(8,128)(2,1)S(1)} collective-permute-done((bf16[1,32,128]{2,1,0:T(8,128)(2,1)}, bf16[1,32,128]{2,1,0:T(8,128)(2,1)S(1)}, u32[]{:S(2)}, u32[]{:S(2)}) %collective-permute-start.4) | collective-permute-done | bytes 8224 | tf_op jit(solution)/shard_map/ppermute | solution.py:22
  13.5 0.7 %pad_maximum_fusion = bf16[4,32,128]{2,1,0:T(8,128)(2,1)S(1)} fusion(bf16[1,32,128]{2,1,0:T(8,128)(2,1)S(1)} %collective-permute-done.4, bf16[1,32,128]{2,1,0:T(8,128)(2,1)S(1)} %collective-permute-done.3, bf16[1,32,128]{2,1,0:T(8,128)(2,1)S(1)} %collective-permute-done.2, bf16[1,32,128]{2,1,0:T(8,128)(2,1)} %bitcast.19), kind=kLoop, calls=%fused_computation | loop fusion | flops 49152 | bytes 65536 | tf_op jit(solution)/shard_map/concatenate | solution.py:33
  14.2 1.5 %collective-permute-start.6 = (bf16[4,32,128]{2,1,0:T(8,128)(2,1)S(1)}, bf16[4,32,128]{2,1,0:T(8,128)(2,1)S(1)}, u32[]{:S(2)}, u32[]{:S(2)}) collective-permute-start(bf16[4,32,128]{2,1,0:T(8,128)(2,1)S(1)} %pad_maximum_fusion), channel_id=1, source_target_pairs={{0,4},{4,0},{8,12},{12,8},{16,20},{20,16},{24,28},{28,24},{1,5},{5... | collective-permute-start | bytes 98312 | tf_op jit(solution)/shard_map/ppermute | solution.py:22
  15.7 0.0 collective-permute-done.refs_0_.refs_1_
  15.7 1.7 %shard_map.86 = (bf16[2048,256]{1,0:T(8,128)(2,1)S(1)}, s32[2048,128]{1,0:T(8,128)S(1)}, f32[2048,128]{1,0:T(8,128)S(1)}, s32[16,128]{1,0:T(8,128)S(1)}, f32[8,2...) custom-call(s32[16,128]{1,0:T(8,128)} %ids_hbm.1, ...), custom_call_target="tpu_custom_call" | custom-call | flops 1073741824 | bytes 2097152 | tf_op jit(solution)/shard_map/pallas_call | solution.py:292
  17.5 1.5 %shard_map.87 = (f32[2048,128]{1,0:T(8,128)S(1)}, f32[2048,128]{1,0:T(8,128)S(1)}) custom-call(f32[1,4]{1,0:T(1,128)S(1)} %get-tuple-element.21.weight_ref, s32[16,128,128]{2,1,0:T(8,128)} %codes_hbm.1, bf16[2048,256]{1,0:T(8,128)(2,1)S(1)} %get-tuple-element.19.onehot_ref, s32[2048,128]{1,0:T(8,128)S(1)} %get-tuple-element.20.high_ref, ...), custom_call_target="tpu_custom_call" | custom-call | flops 1073741824 | bytes 2097152 | tf_op jit(solution)/shard_map/pallas_call | solution.py:328
  19.0 0.0 collective-permute-done.5.refs_3_
  19.0 1.3 %shard_map.88 = (f32[8,128]{1,0:T(8,128)S(1)}, bf16[2048,128]{1,0:T(8,128)(2,1)S(1)}) custom-call(s32[16,128]{1,0:T(8,128)S(1)} %get-tuple-element.17.live_ref, f32[8,256]{1,0:T(8,128)S(1)} %get-tuple-element.18.mine_ref, bf16[2048,256]{1,0:T(8,128)(2,1)S(1)} %get-tuple-element.19.onehot_ref, s32[2048,128]{1,0:T(8,128)S(1)} %get-tuple-element.20.high_ref, ...), custom_call_target="tpu_custom_call" | custom-call | flops 1073741824 | bytes 2097152 | tf_op jit(solution)/shard_map/pallas_call | solution.py:352
  20.3 0.0 collective-permute-done.6
  20.3 0.8 %shard_map.89 = f32[8,128]{1,0:T(8,128)S(1)} custom-call(s32[16,128]{1,0:T(8,128)S(1)} %get-tuple-element.17.live_ref, f32[8,256]{1,0:T(8,128)S(1)} %get-tuple-element.18.mine_ref, bf16[2048,128]{1,0:T(8,128)(2,1)S(1)} %get-tuple-element.26.embedded_ref, f32[8,128]{1,0:T(8,128)S(1)} %get-tuple-element.27.early_ref, bf16[128,128]{1,0:T(8,128)(2,1)S(1)} %bitcast.15, ...), custom_call_target="tpu_custom_call" | custom-call | flops 1073741824 | bytes 2097152 | tf_op jit(solution)/shard_map/pallas_call | solution.py:361
  21.1 8.9 %all_to_all.11 = f32[8,1,128]{2,1,0:T(1,128)S(1)} all-to-all(f32[8,1,128]{2,1,0:T(1,128)S(1)} %bitcast.14), channel_id=1, replica_groups=mesh['shard'=8,'rep'=4] {'shard'}, dimensions={0} | all-to-all | bytes 8192 | tf_op jit(solution)/shard_map/all_to_all | solution.py:369
  30.0 0.6 %shard_map.90 = (f32[1,32]{1,0:T(1,128)}, f32[1,64]{1,0:T(1,128)}) custom-call(f32[8,128]{1,0:T(8,128)S(1)} %bitcast.13, f32[8,128]{1,0:T(8,128)S(1)} %get-tuple-element.28.owner_ref, s32[8,128]{1,0:T(8,128)S(1)} %get-tuple-element.29.column_ref), custom_call_target="tpu_custom_call" | custom-call | tf_op jit(solution)/shard_map/pallas_call | solution.py:370
Async XLA Ops:
  0.6 9.6 %collective-permute-start.1 = (bf16[1024,128]{1,0:T(8,128)(2,1)}, bf16[1024,128]{1,0:T(8,128)(2,1)S(1)}, u32[]{:S(2)}, u32[]{:S(2)}) collective-permute-start(bf16[1024,128]{1,0:T(8,128)(2,1)} %own_hbm.1), channel_id=1, source_target_pairs={{0,2},{1,3},{2,0},{3,1},{4,6},{5,7},{6,4},{7,5},{8,10},{9,11},{10,... | collective-permute-start | bytes 786440 | tf_op jit(solution)/shard_map/ppermute | solution.py:22
  3.7 12.1 %collective-permute-start = (bf16[1024,128]{1,0:T(8,128)(2,1)}, bf16[1024,128]{1,0:T(8,128)(2,1)S(1)}, u32[]{:S(2)}, u32[]{:S(2)}) collective-permute-start(bf16[1024,128]{1,0:T(8,128)(2,1)} %own_hbm.1), channel_id=1, source_target_pairs={{0,1},{1,0},{2,3},{3,2},{4,5},{5,4},{6,7},{7,6},{8,9},{9,8},{10,11... | collective-permute-start | bytes 786440 | tf_op jit(solution)/shard_map/ppermute | solution.py:22
  3.7 6.5 %collective-permute-start.2 = (bf16[1,32,128]{2,1,0:T(8,128)(2,1)}, bf16[1,32,128]{2,1,0:T(8,128)(2,1)S(1)}, u32[]{:S(2)}, u32[]{:S(2)}) collective-permute-start(bf16[1,32,128]{2,1,0:T(8,128)(2,1)} %bitcast.16), channel_id=1, source_target_pairs={{0,8},{4,12},{8,0},{12,4},{16,24},{20,28},{24,16},{28,20},{1,9},{5... | collective-permute-start | bytes 24584 | tf_op jit(solution)/shard_map/ppermute | solution.py:22
  5.2 4.9 %collective-permute-start.3 = (bf16[1,32,128]{2,1,0:T(8,128)(2,1)}, bf16[1,32,128]{2,1,0:T(8,128)(2,1)S(1)}, u32[]{:S(2)}, u32[]{:S(2)}) collective-permute-start(bf16[1,32,128]{2,1,0:T(8,128)(2,1)} %bitcast.17), channel_id=1, source_target_pairs={{0,16},{4,20},{8,24},{12,28},{16,0},{20,4},{24,8},{28,12},{1,17},{... | collective-permute-start | bytes 24584 | tf_op jit(solution)/shard_map/ppermute | solution.py:22
  7.8 5.7 %collective-permute-start.4 = (bf16[1,32,128]{2,1,0:T(8,128)(2,1)}, bf16[1,32,128]{2,1,0:T(8,128)(2,1)S(1)}, u32[]{:S(2)}, u32[]{:S(2)}) collective-permute-start(bf16[1,32,128]{2,1,0:T(8,128)(2,1)} %bitcast.18), channel_id=1, source_target_pairs={{0,24},{4,28},{8,16},{12,20},{16,8},{20,12},{24,0},{28,4},{1,25},{... | collective-permute-start | bytes 24584 | tf_op jit(solution)/shard_map/ppermute | solution.py:22
  10.2 8.8 %collective-permute-start.5 = (bf16[1024,128]{1,0:T(8,128)(2,1)S(1)}, bf16[1024,128]{1,0:T(8,128)(2,1)S(1)}, u32[]{:S(2)}, u32[]{:S(2)}) collective-permute-start(bf16[1024,128]{1,0:T(8,128)(2,1)S(1)} %collective-permute-done.1.refs_1_.refs_2_), channel_id=1, source_target_pairs={{0,1},{1,0},{2,3},{3,2},{4,5},{5,4},{6,7},{7,6},{8,9},{9,8},{10,11... | collective-permute-start | bytes 786440 | tf_op jit(solution)/shard_map/ppermute | solution.py:22
  14.2 6.1 %collective-permute-start.6 = (bf16[4,32,128]{2,1,0:T(8,128)(2,1)S(1)}, bf16[4,32,128]{2,1,0:T(8,128)(2,1)S(1)}, u32[]{:S(2)}, u32[]{:S(2)}) collective-permute-start(bf16[4,32,128]{2,1,0:T(8,128)(2,1)S(1)} %pad_maximum_fusion), channel_id=1, source_target_pairs={{0,4},{4,0},{8,12},{12,8},{16,20},{20,16},{24,28},{28,24},{1,5},{5... | collective-permute-start | bytes 98312 | tf_op jit(solution)/shard_map/ppermute | solution.py:22
